TPU v7x, 32 devices: a whole 2x2x4 slice. The times are simulated.
32 devices in a mesh: dp: 8 (over z, y), rows: 4 (over x, core).
Axes of the slice: x: 2, y: 2, z: 4, core: 2. Of those that a mesh axis runs over, the one named last changes fastest.
Arguments:
- x_views: bfloat16 [128, 2, 8, 7, 2048], P('dp', None, 'rows'), may hold values from -6 to 6
- x_crops: bfloat16 [128, 4, 4, 3, 2048], P('dp', None, 'rows'), may hold values from -6 to 6
- mask_views: int32 [128, 2, 8], P('dp', None, 'rows'), may hold values from 0 to 1, as said below
- mask_crops: int32 [128, 4, 4], P('dp', None, 'rows'), may hold values from 0 to 1, as said below
- w_reduce: float32 [2048, 512], P(('dp', 'rows')), may hold values from -0.125 to 0.125
- w_spatial: float32 [3, 3, 512, 512], P(None, None, ('dp', 'rows')), may hold values from -0.09375 to 0.09375
- w_expand: float32 [512, 2048], P(('dp', 'rows')), may hold values from -0.25 to 0.25
- gain_reduce: float32 [512], P(('dp', 'rows')), may hold values from 0.5 to 2
- shift_reduce: float32 [512], P(('dp', 'rows')), may hold values from -0.5 to 0.5
- gain_spatial: float32 [512], P(('dp', 'rows')), may hold values from 0.5 to 2
- shift_spatial: float32 [512], P(('dp', 'rows')), may hold values from -0.5 to 0.5
- gain_expand: float32 [2048], P(('dp', 'rows')), may hold values from 0.5 to 2
- shift_expand: float32 [2048], P(('dp', 'rows')), may hold values from -0.5 to 0.5
- cot_views: bfloat16 [128, 2, 8, 7, 2048], P('dp', None, 'rows'), may hold values from -6 to 6
- cot_crops: bfloat16 [128, 4, 4, 3, 2048], P('dp', None, 'rows'), may hold values from -6 to 6
- cot_pool_views: float32 [128, 2, 2048], P('dp'), may hold values from -48 to 48
- cot_pool_crops: float32 [128, 4, 2048], P('dp'), may hold values from -48 to 48
Outputs:
- out_views: float32 [128, 2, 8, 7, 2048], P('dp', None, 'rows')
- out_crops: float32 [128, 4, 4, 3, 2048], P('dp', None, 'rows')
- pool_views: float32 [128, 2, 2048], P('dp')
- pool_crops: float32 [128, 4, 2048], P('dp')
- grad_views: float32 [128, 2, 8, 7, 2048], P('dp', None, 'rows')
- grad_crops: float32 [128, 4, 4, 3, 2048], P('dp', None, 'rows')
- grad_w_reduce: float32 [2048, 512], P(('dp', 'rows'))
- grad_w_spatial: float32 [3, 3, 512, 512], P(None, None, ('dp', 'rows'))
- grad_w_expand: float32 [512, 2048], P(('dp', 'rows'))
- grad_gain_reduce: float32 [512], P(('dp', 'rows'))
- grad_shift_reduce: float32 [512], P(('dp', 'rows'))
- grad_gain_spatial: float32 [512], P(('dp', 'rows'))
- grad_shift_spatial: float32 [512], P(('dp', 'rows'))
- grad_gain_expand: float32 [2048], P(('dp', 'rows'))
- grad_shift_expand: float32 [2048], P(('dp', 'rows'))
Inputs may be any that keep to these rules, and one draw needn't show every extreme that they name: `mask_views`: each view has exactly one padding row, its first or its last of 8; all other rows are 1. `mask_crops`: each crop has exactly one padding row, its first or its last of 4; all other rows are 1.
All inputs are finite; a program needn't handle non-finite values.
Results may differ from a plain program's by a relative error of at most 0.02.
Values may be sent and summed in bfloat16 or wider, within the bound.
A program may use at most 192 MiB of HBM per device.

v0:
```python
import functools

import jax
import jax.numpy as jnp
from jax import lax
from jax.experimental import pallas as pl
from jax.experimental.pallas import tpu as pltpu
from jax.sharding import PartitionSpec as P

MESH = pl.DeviceIdType.MESH
ALL = slice(None)
BF = jnp.bfloat16
F32 = jnp.float32
eps = 1e-05
TILE = 256


def lanes(j, width=TILE):
    if isinstance(j, int):
        return slice(j * width, (j + 1) * width)
    return pl.ds(pl.multiple_of(j * width, width), width)


def half(h, width):
    return ALL if h is None else slice(h * (width // 2), (h + 1) * (width // 2))


def dot(a, b):
    return lax.dot_general(a, b, (((1,), (0,)), ((), ())), preferred_element_type=F32)


def dot_t(a, b):
    return lax.dot_general(a, b, (((1,), (1,)), ((), ())), preferred_element_type=F32)


def dot_r(a, b):
    return lax.dot_general(a, b, (((0,), (0,)), ((), ())), preferred_element_type=F32)


def sigmoid(v):
    return 0.5 * jnp.tanh(0.5 * v) + 0.5


class Place:
    def __init__(self, n_dp, n_rows):
        self.ny, self.nc = 2, 2
        self.nz, self.nx = n_dp // 2, n_rows // 2
        self.n_dp, self.n_rows = n_dp, n_rows
        self.dp, self.r = lax.axis_index("dp"), lax.axis_index("rows")
        self.z, self.y = self.dp // 2, self.dp % 2
        self.x, self.c = self.r // 2, self.r % 2

    def dev(self, z, y, x, c):
        return {"dp": z * self.ny + y, "rows": x * self.nc + c}


def remote(src, dst, ssem, rsem, to):
    return pltpu.make_async_remote_copy(
        src_ref=src, dst_ref=dst, send_sem=ssem, recv_sem=rsem, device_id=to, device_id_type=MESH
    )


class Gather:
    def __init__(self, me, view, ssem, rsem, halves=(0, 1)):
        self.me, self.view, self.s, self.r, self.halves = me, view, ssem, rsem, halves

    def cp(self, k, place, to):
        ref = self.view(*place)
        return remote(ref, ref, self.s.at[k], self.r.at[k], self.me.dev(*to))

    def along_z(self, dz, recv):
        me = self.me
        if recv:
            z = (me.z + me.nz - dz) % me.nz
            return self.cp(dz - 1, (z, me.y, me.x, me.c, None), (z, me.y, me.x, me.c))
        to = ((me.z + dz) % me.nz, me.y, me.x, me.c)
        return self.cp(dz - 1, (me.z, me.y, me.x, me.c, None), to)

    def second(self, h, recv):
        me = self.me
        yy, xx = (1 - me.y, me.x) if h == 0 else (me.y, 1 - me.x)
        place = (ALL, yy, xx, me.c, h) if recv else (ALL, me.y, me.x, me.c, h)
        return self.cp(3 + h, place, (me.z, yy, xx, me.c))

    def third(self, h, recv):
        me = self.me
        if h == 0:
            return self.cp(
                5, (ALL, ALL, 1 - me.x if recv else me.x, me.c, h), (me.z, me.y, 1 - me.x, me.c)
            )
        return self.cp(
            6, (ALL, 1 - me.y if recv else me.y, ALL, me.c, h), (me.z, 1 - me.y, me.x, me.c)
        )

    def core(self, k, recv):
        me = self.me
        c = 1 - me.c if recv else me.c
        place = (
            (ALL, me.y, me.x, c, None),
            (ALL, 1 - me.y, me.x, c, 0),
            (ALL, me.y, 1 - me.x, c, 1),
            (ALL, ALL, 1 - me.x, c, 0),
            (ALL, 1 - me.y, ALL, c, 1),
        )[k]
        return self.cp(7 + k, place, (me.z, me.y, me.x, 1 - me.c))

    def start(self):
        for dz in range(1, self.me.nz):
            self.along_z(dz, False).start()

    def got_z(self):
        for dz in range(1, self.me.nz):
            self.along_z(dz, True).wait_recv()

    def stage2(self):
        for h in self.halves:
            self.second(h, False).start()
        self.core(0, False).start()

    def stage3(self):
        for h in self.halves:
            self.second(h, True).wait_recv()
            self.third(h, False).start()
            self.core(1 + h, False).start()

    def stage4(self):
        for h in self.halves:
            self.third(h, True).wait_recv()
            self.core(3 + h, False).start()

    def finish(self):
        self.core(0, True).wait_recv()
        for h in self.halves:
            self.core(1 + h, True).wait_recv()
            self.core(3 + h, True).wait_recv()

    def drain(self):
        for dz in range(1, self.me.nz):
            self.along_z(dz, False).wait_send()
        self.core(0, False).wait_send()
        for h in self.halves:
            self.second(h, False).wait_send()
            self.third(h, False).wait_send()
            self.core(1 + h, False).wait_send()
            self.core(3 + h, False).wait_send()


class Reduce:
    def __init__(self, me, view, from_core, from_third, from_second, from_z, ssem, rsem):
        self.me, self.view, self.s, self.r = me, view, ssem, rsem
        self.fc, self.f3, self.f2, self.fz = from_core, from_third, from_second, from_z

    def core(self):
        me = self.me
        return remote(
            self.view(ALL, ALL, ALL, 1 - me.c, None),
            self.fc(ALL, ALL, ALL, None),
            self.s.at[0],
            self.r.at[0],
            me.dev(me.z, me.y, me.x, 1 - me.c),
        )

    def third(self, h):
        me = self.me
        place = (ALL, ALL, 1 - me.x) if h == 0 else (ALL, 1 - me.y, ALL)
        to = (me.z, me.y, 1 - me.x, me.c) if h == 0 else (me.z, 1 - me.y, me.x, me.c)
        return remote(
            self.view(*place, me.c, h), self.f3(h), self.s.at[1 + h], self.r.at[1 + h], me.dev(*to)
        )

    def second(self, h):
        me = self.me
        place = (ALL, 1 - me.y, me.x) if h == 0 else (ALL, me.y, 1 - me.x)
        to = (me.z, 1 - me.y, me.x, me.c) if h == 0 else (me.z, me.y, 1 - me.x, me.c)
        return remote(
            self.view(*place, me.c, h), self.f2(h), self.s.at[3 + h], self.r.at[3 + h], me.dev(*to)
        )

    def along_z(self, dz):
        me = self.me
        z = (me.z + dz) % me.nz
        return remote(
            self.view(z, me.y, me.x, me.c, None),
            self.fz(dz - 1),
            self.s.at[4 + dz],
            self.r.at[4 + dz],
            me.dev(z, me.y, me.x, me.c),
        )

    def start(self):
        self.core().start()

    def stage2(self):
        me = self.me
        self.core().wait_recv()
        for h in (0, 1):
            first = (ALL, ALL, 1 - me.x) if h == 0 else (ALL, 1 - me.y, ALL)
            ref = self.view(*first, me.c, h)
            ref[...] = ref[...] + self.fc(*first, h)[...]
            self.third(h).start()
        for h in (0, 1):
            rest = (ALL, ALL, me.x) if h == 0 else (ALL, me.y, ALL)
            ref = self.view(*rest, me.c, h)
            ref[...] = ref[...] + self.fc(*rest, h)[...]

    def stage3(self):
        me = self.me
        for h in (0, 1):
            self.third(h).wait_recv()
            kept = (ALL, ALL, me.x) if h == 0 else (ALL, me.y, ALL)
            ref = self.view(*kept, me.c, h)
            ref[...] = ref[...] + self.f3(h)[...]
            self.second(h).start()

    def stage4(self):
        me = self.me
        for h in (0, 1):
            self.second(h).wait_recv()
            ref = self.view(ALL, me.y, me.x, me.c, h)
            ref[...] = ref[...] + self.f2(h)[...]
        for dz in range(1, me.nz):
            self.along_z(dz).start()

    def finish(self):
        me = self.me
        total = self.view(me.z, me.y, me.x, me.c, None)[...].astype(F32)
        for dz in range(1, me.nz):
            self.along_z(dz).wait_recv()
            total = total + self.fz(dz - 1)[...].astype(F32)
        return total

    def drain(self):
        self.core().wait_send()
        for h in (0, 1):
            self.third(h).wait_send()
            self.second(h).wait_send()
        for dz in range(1, self.me.nz):
            self.along_z(dz).wait_send()


def kernel(n_dp, n_rows, sizes, *refs):
    (
        xv_h, xc_h, cv_h, cc_h, cpv_h, cpc_h, mv_in, mc_in, wr_in, ws_in, we_in,
        g1_in, s1_in, g2_in, s2_in, g3_in, s3_in,
        yv_h, yc_h, gv_h, gc_h, poolv_o, poolc_o, gwr_o, gws_o, gwe_o, small_o,
        wr, ws, we, par, mask, raw_v, raw_c, cpv, cpc, x, xt, cot, a1, a2, a3, gpre, ysv, ysc, gact,
        hv, hc, dv, dc, h2, h2t, ga1, gwr, gws, gwe,
        fc_we, fc_ws, fc_wr, f3_we, f3_ws, f3_wr, f2_we, f2_ws, f2_wr, fz_we, fz_ws, fz_wr,
        p1, p3, mi1, mi2, mi3, cnt, ex1, ex2, ex3, bx1, bx2, bx3, tot1, tot2, tot3,
        pf, pb, pr, sb, rb,
        in_sem, out_sem, ag_s, ag_r, rs_s, rs_r, ex_s, ex_r, halo_s, halo_r, pool_s, pool_r, sm_s, sm_r,
    ) = refs
    (maps_v, cols_v, maps_c, cols_c, valid_v, valid_c) = sizes
    me = Place(n_dp, n_rows)
    mid, wide = a1.shape[1], a3.shape[1]
    pix_v = 2 * cols_v * maps_v
    pix = a1.shape[0]
    row_v, row_c = cols_v * maps_v, cols_c * maps_c
    count = (float(maps_v * valid_v), float(maps_c * valid_c))
    CH = 32
    chunks = [(s, 0 if s < pix_v else 1) for s in range(0, pix, CH)]

    def fetch(k, views, crops):
        return [
            pltpu.make_async_copy(views.at[:, col], raw_v.at[col], in_sem.at[k, col]) for col in range(cols_v)
        ] + [pltpu.make_async_copy(crops, raw_c, in_sem.at[k, cols_v])]

    def arrange(out):
        def body(j, carry):
            cols = lanes(j)
            for col in range(cols_v):
                for r in (0, 1):
                    at = r * row_v + col * maps_v
                    out[at : at + maps_v, cols] = raw_v[col, :, r, cols]
            for col in range(cols_c):
                at = pix_v + col * maps_c
                out[at : at + maps_c, cols] = raw_c[:, col, :, cols].reshape(maps_c, TILE)
            return carry

        lax.fori_loop(0, wide // TILE, body, 0)

    x_copies, cot_copies = fetch(0, xv_h, xc_h), fetch(1, cv_h, cc_h)
    pool_copies = [
        pltpu.make_async_copy(cpv_h, cpv, in_sem.at[2, 0]),
        pltpu.make_async_copy(cpc_h, cpc, in_sem.at[2, 1]),
    ]
    for cp in x_copies + pool_copies:
        cp.start()

    here = (me.z, me.y, me.x, me.c)
    wr[here] = wr_in[...].astype(BF)
    ws[(ALL,) + here] = ws_in[...].astype(BF)
    we[here] = we_in[...].astype(BF)
    own = par.at[here]
    own[...] = jnp.zeros(own.shape, F32)
    for i, ref in enumerate((g1_in, s1_in, g2_in, s2_in, g3_in, s3_in)):
        own[i : i + 1, 0 : ref.shape[1]] = ref[...].astype(BF).astype(F32)

    def mask_column(row_of, per, maps):
        lane = lax.broadcasted_iota(jnp.int32, (maps, 16), 1)
        place = lax.broadcasted_iota(jnp.int32, (maps, 16), 0)
        total = jnp.zeros((maps, 16), F32)
        for k in range(per):
            hit = jnp.logical_and(place % per == k, lane == place // per)
            total = total + jnp.where(hit, row_of(k).astype(F32), 0.0)
        return jnp.broadcast_to(jnp.sum(total, axis=1, keepdims=True), (maps, 128))

    for r in (0, 1):
        column = mask_column(lambda k: mv_in[k, r : r + 1, :], mv_in.shape[0], maps_v)
        for col in range(cols_v):
            at = r * row_v + col * maps_v
            mask[at : at + maps_v] = column
    column = mask_column(lambda k: mc_in[k], mc_in.shape[0], maps_c)
    for col in range(cols_c):
        at = pix_v + col * maps_c
        mask[at : at + maps_c] = column

    cnt_own = cnt.at[me.r]
    cnt_own[0:1] = jnp.sum(mask[0:pix_v], axis=0, keepdims=True)
    cnt_own[1:2] = jnp.sum(mask[pix_v:pix], axis=0, keepdims=True)
    cnt_own[2:8] = jnp.zeros((6, 128), F32)

    barrier = pltpu.get_barrier_semaphore()
    peers = [{"dp": me.dp, "rows": (me.r + d) % n_rows} for d in range(1, n_rows)]
    peers += [{"dp": (me.dp + d) % n_dp, "rows": me.r} for d in range(1, n_dp)]
    for peer in peers:
        pl.semaphore_signal(barrier, inc=1, device_id=peer, device_id_type=MESH)
    pl.semaphore_wait(barrier, len(peers))

    def piece(k, view, halves=(0, 1)):
        return Gather(me, view, ag_s.at[k], ag_r.at[k], halves)

    small_piece = piece(0, lambda z, y, x, c, h: par.at[z, y, x, c], (0,))
    pieces = [piece(1, lambda z, y, x, c, h: wr.at[z, y, x, c, :, half(h, mid)])]
    for i in range(3):
        pieces.append(
            piece(2 + i, lambda z, y, x, c, h, i=i: ws.at[3 * i : 3 * i + 3, z, y, x, c, :, half(h, mid)])
        )
    pieces.append(piece(5, lambda z, y, x, c, h: we.at[z, y, x, c, :, half(h, wide)]))

    def exchange(k, buf):
        def cp(d, recv):
            peer = (me.r + n_rows - d) % n_rows if recv else (me.r + d) % n_rows
            ref = buf.at[peer if recv else me.r]
            return remote(ref, ref, ex_s.at[k, d - 1], ex_r.at[k, d - 1], {"dp": me.dp, "rows": peer})

        def send():
            for d in range(1, n_rows):
                cp(d, False).start()

        def wait():
            for d in range(1, n_rows):
                cp(d, True).wait_recv()

        def drain():
            for d in range(1, n_rows):
                cp(d, False).wait_send()

        return send, wait, drain

    exchanges = [exchange(k, b) for k, b in enumerate((cnt, ex1, ex2, ex3, bx1, bx2, bx3))]

    def rim(k, v, c):
        def cps(up):
            peer = {"dp": me.dp, "rows": (me.r + n_rows - 1) % n_rows if up else (me.r + 1) % n_rows}
            base = 0 if up else 2
            vs, vd = (1, 3) if up else (2, 0)
            csrc, cd = (1, 2) if up else (1, 0)
            return [
                remote(
                    v.at[vs, maps_v : maps_v + row_v],
                    v.at[vd, maps_v : maps_v + row_v],
                    halo_s.at[k, base],
                    halo_r.at[k, base],
                    peer,
                ),
                remote(
                    c.at[csrc, maps_c : maps_c + row_c],
                    c.at[cd, maps_c : maps_c + row_c],
                    halo_s.at[k, base + 1],
                    halo_r.at[k, base + 1],
                    peer,
                ),
            ]

        def each(up, fn):
            def body():
                for cp in cps(up):
                    fn(cp)

            return body

        first, last = me.r == 0, me.r == n_rows - 1

        def send():
            pl.when(jnp.logical_not(first))(each(True, lambda cp: cp.start()))
            pl.when(jnp.logical_not(last))(each(False, lambda cp: cp.start()))

        def wait():
            pl.when(jnp.logical_not(last))(each(True, lambda cp: cp.wait_recv()))
            pl.when(jnp.logical_not(first))(each(False, lambda cp: cp.wait_recv()))

        def drain():
            pl.when(jnp.logical_not(first))(each(True, lambda cp: cp.wait_send()))
            pl.when(jnp.logical_not(last))(each(False, lambda cp: cp.wait_send()))

        return send, wait, drain

    rim_h, rim_d = rim(0, hv, hc), rim(1, dv, dc)

    def clear_rims(v, c):
        zv, zc = jnp.zeros((maps_v, mid), BF), jnp.zeros((maps_c, mid), BF)
        for r in range(4):
            v[r, 0:maps_v] = zv
            v[r, maps_v + row_v : 2 * maps_v + row_v] = zv
        for r in range(3):
            c[r, 0:maps_c] = zc
            c[r, maps_c + row_c : 2 * maps_c + row_c] = zc

        @pl.when(me.r == 0)
        def _():
            v[0, maps_v : maps_v + row_v] = jnp.zeros((row_v, mid), BF)
            c[0, maps_c : maps_c + row_c] = jnp.zeros((row_c, mid), BF)

        @pl.when(me.r == n_rows - 1)
        def _():
            v[3, maps_v : maps_v + row_v] = jnp.zeros((row_v, mid), BF)
            c[2, maps_c : maps_c + row_c] = jnp.zeros((row_c, mid), BF)

    def tile_rows(ref, j):
        per = me.nz * TILE // mid
        return ref[j * per : (j + 1) * per]

    def fold(v):
        return jnp.sum(v.reshape(v.shape[0] // 8, 8, v.shape[1]), axis=0)

    def put(buf, j, k, value):
        tiles = buf.shape[2] // TILE
        if isinstance(j, int):
            buf[me.r, 4 * (j // tiles) + k : 4 * (j // tiles) + k + 1, lanes(j % tiles)] = value
        else:
            buf[me.r, pl.ds(4 * (j // tiles) + k, 1), lanes(j % tiles)] = value

    def local_stats(a, buf, n_tiles):
        def body(j, carry):
            cols = lanes(j)
            for grp in (0, 1):
                acc = jnp.zeros((8, TILE), F32)
                for s, g in chunks:
                    if g == grp:
                        acc = acc + fold(a[s : s + CH, cols] * mask[s : s + CH, 0:1])
                total = jnp.sum(acc, axis=0, keepdims=True)
                n_own = jnp.maximum(cnt[me.r, grp : grp + 1, 0:1], 1.0)
                mean = total / n_own
                acc = jnp.zeros((8, TILE), F32)
                for s, g in chunks:
                    if g == grp:
                        d = (a[s : s + CH, cols] - mean) * mask[s : s + CH, 0:1]
                        acc = acc + fold(d * d)
                put(buf, j, 2 * grp, total)
                put(buf, j, 2 * grp + 1, jnp.sum(acc, axis=0, keepdims=True))
            return carry

        for j in range(n_tiles):
            body(j, 0) if n_tiles <= 2 else None
        if n_tiles > 2:
            lax.fori_loop(0, n_tiles, body, 0)

    def merge_stats(buf, mi):
        width = buf.shape[2]
        for hf in (0, 1):
            for grp in (0, 1):
                k = 4 * hf + 2 * grp
                total = sum(buf[i, k : k + 1] for i in range(n_rows))
                mean = total / count[grp]
                spread = jnp.zeros_like(mean)
                for i in range(n_rows):
                    n_i = cnt[i, grp : grp + 1, 0:1]
                    off = buf[i, k : k + 1] / jnp.maximum(n_i, 1.0) - mean
                    spread = spread + buf[i, k + 1 : k + 2] + n_i * (off * off)
                mi[2 * grp : 2 * grp + 1, hf * width : (hf + 1) * width] = mean
                mi[2 * grp + 1 : 2 * grp + 2, hf * width : (hf + 1) * width] = lax.rsqrt(
                    spread / count[grp] + eps
                )

    def merge_grads(buf, tot):
        width = buf.shape[2]
        for hf in (0, 1):
            block = buf[0, 4 * hf : 4 * hf + 4]
            for i in range(1, n_rows):
                block = block + buf[i, 4 * hf : 4 * hf + 4]
            tot[0:4, hf * width : (hf + 1) * width] = block

    def expand_params():
        blocks = par[...].reshape(n_dp * n_rows * 8, 128).astype(BF)
        n_dev = n_dp * n_rows
        for out, width in ((p1, mid), (p3, wide)):
            share = width // n_dev
            step = 512
            for t in range(width // step):
                lane = lax.broadcasted_iota(jnp.int32, (128, step), 1) + t * step
                place = lax.broadcasted_iota(jnp.int32, (128, step), 0)
                pick = jnp.where(lane % share == place, 1.0, 0.0).astype(BF)
                spread = dot(blocks, pick).reshape(n_dev, 8, step)
                owner = (lax.broadcasted_iota(jnp.int32, (8, step), 1) + t * step) // share
                total = jnp.zeros((8, step), F32)
                for d in range(n_dev):
                    total = total + jnp.where(owner == d, spread[d], 0.0)
                out[:, t * step : (t + 1) * step] = total

    def gain(out, i, cols):
        return out[i : i + 1, cols]

    small_piece.start()
    pieces[0].start()
    exchanges[0][0]()
    clear_rims(hv, hc)
    clear_rims(dv, dc)
    for cp in x_copies:
        cp.wait()

    def step0(t):
        pieces[t].got_z()
        if t + 1 < len(pieces):
            pieces[t + 1].start()
        pieces[t].stage2()

    arrange(x)
    for cp in cot_copies:
        cp.start()
    small_piece.got_z()
    small_piece.stage2()
    step0(0)
    for t in range(wide // TILE):
        xt[t * TILE : (t + 1) * TILE, :] = x[:, t * TILE : (t + 1) * TILE].T
    small_piece.stage3()
    step0(1)
    pieces[0].stage3()
    small_piece.stage4()
    for cp in cot_copies:
        cp.wait()
    arrange(cot)
    step0(2)
    pieces[1].stage3()
    pieces[0].stage4()
    small_piece.finish()
    expand_params()
    step0(3)
    pieces[2].stage3()
    pieces[1].stage4()
    pieces[0].finish()
    exchanges[0][1]()

    def conv1(j, carry):
        w = wr[:, :, :, :, :, lanes(j)].reshape(wide, TILE)
        a1[:, lanes(j)] = dot(x[...], w)
        return carry

    lax.fori_loop(0, mid // TILE, conv1, 0)
    local_stats(a1, ex1, mid // TILE)
    exchanges[1][0]()
    step0(4)
    pieces[3].stage3()
    pieces[2].stage4()
    pieces[1].finish()
    exchanges[1][1]()
    merge_stats(ex1, mi1)

    def store_rows(v, c, s, cols, value):
        if s < pix_v:
            r, o = s // row_v, s % row_v
            v[1 + r, maps_v + o : maps_v + o + CH, cols] = value
        else:
            o = s - pix_v
            c[1, maps_c + o : maps_c + o + CH, cols] = value

    def act(a, mi, i, store):
        def body(j, carry):
            cols = lanes(j)
            scale = [mi[2 * g + 1 : 2 * g + 2, cols] * gain(p1, i, cols) for g in (0, 1)]
            mean = [mi[2 * g : 2 * g + 1, cols] for g in (0, 1)]
            shift = gain(p1, i + 1, cols)
            for s, g in chunks:
                zed = (a[s : s + CH, cols] - mean[g]) * scale[g] + shift
                store(s, cols, (zed * sigmoid(zed) * mask[s : s + CH, 0:1]).astype(BF))
            return carry

        for j in range(mid // TILE):
            body(j, 0)

    act(a1, mi1, 0, lambda s, cols, value: store_rows(hv, hc, s, cols, value))
    rim_h[0]()
    pieces[4].stage3()
    pieces[3].stage4()
    pieces[2].finish()
    pieces[4].stage4()
    pieces[3].finish()
    rim_h[1]()

    def conv2(tap, carry):
        dy, dx = tap // 3, tap % 3
        w = ws[tap].reshape(mid, mid)
        for r in (0, 1):
            left = hv[r + dy, pl.ds(pl.multiple_of(dx * maps_v, maps_v), row_v), :]
            block = a2.at[r * row_v : (r + 1) * row_v]
            block[...] = block[...] + dot(left, w)
        left = hc[dy, pl.ds(pl.multiple_of(dx * maps_c, maps_c), row_c), :]
        block = a2.at[pix_v:pix]
        block[...] = block[...] + dot(left, w)
        return carry

    a2[...] = jnp.zeros(a2.shape, F32)
    lax.fori_loop(0, 9, conv2, 0)
    local_stats(a2, ex2, mid // TILE)
    exchanges[2][0]()
    exchanges[2][1]()
    merge_stats(ex2, mi2)

    def store_h2(s, cols, value):
        h2[s : s + CH, cols] = value

    act(a2, mi2, 2, store_h2)
    pieces[4].finish()
    for cp in pool_copies:
        cp.wait()

    def conv3(j, carry):
        w = we[:, :, :, :, :, lanes(j)].reshape(mid, TILE)
        a3[:, lanes(j)] = dot(h2[...], w)
        return carry

    lax.fori_loop(0, wide // TILE, conv3, 0)
    local_stats(a3, ex3, wide // TILE)
    exchanges[3][0]()
    h2t[...] = h2[...].T
    exchanges[3][1]()
    merge_stats(ex3, mi3)

    def out_copies(j, slot, views, crops):
        return [
            pltpu.make_async_copy(ysv.at[slot], views.at[:, :, :, lanes(j)], out_sem.at[slot, 0]),
            pltpu.make_async_copy(ysc.at[slot], crops.at[:, :, j], out_sem.at[slot, 1]),
        ]

    def store_out(slot, s, value):
        if s < pix_v:
            ysv[slot, :, s % row_v // maps_v, s // row_v, :] = value
        else:
            col, at = (s - pix_v) // maps_c, (s - pix_v) % maps_c
            for k in (0, 1):
                ysc[slot, at : at + CH, col, k, :] = value[:, k * 128 : (k + 1) * 128]

    def last(jj, carry):
        for slot in (0, 1):
            j = 2 * jj + slot
            cols = lanes(j)

            @pl.when(jj > 0)
            def _():
                for cp in out_copies(j, slot, yv_h, yc_h):
                    cp.wait()

            mean = [mi3[2 * g : 2 * g + 1, cols] for g in (0, 1)]
            inv = [mi3[2 * g + 1 : 2 * g + 2, cols] for g in (0, 1)]
            gn, sh = gain(p3, 4, cols), gain(p3, 5, cols)
            sums = [jnp.zeros((8, TILE), F32) for _ in range(4)]
            pooled = [jnp.zeros((CH, TILE), F32) for _ in range((maps_v + maps_c) // CH)]
            per_v, per_c = CH // cpv.shape[1], CH // cpc.shape[1]
            cps = [
                cpv[s : s + per_v, :, cols].reshape(CH, TILE) * (1.0 / valid_v)
                for s in range(0, cpv.shape[0], per_v)
            ] + [
                cpc[s : s + per_c, :, cols].reshape(CH, TILE) * (1.0 / valid_c)
                for s in range(0, cpc.shape[0], per_c)
            ]
            for s, g in chunks:
                which = (s % maps_v) // CH if g == 0 else (maps_v + (s - pix_v) % maps_c) // CH
                rows = slice(s, s + CH)
                m = mask[rows, 0:1]
                nh = (a3[rows, cols] - mean[g]) * inv[g]
                pre = x[rows, cols].astype(F32) + (nh * gn + sh)
                sig = sigmoid(pre)
                out = pre * sig * m
                store_out(slot, s, out)
                pooled[which] = pooled[which] + out
                gp = (cot[rows, cols].astype(F32) + cps[which]) * m * (sig * (1.0 + pre * (1.0 - sig)))
                gpre[rows, cols] = gp
                sums[2 * g] = sums[2 * g] + fold(gp * nh)
                sums[2 * g + 1] = sums[2 * g + 1] + fold(gp)
            for k in range(4):
                put(bx3, j, k, jnp.sum(sums[k], axis=0, keepdims=True))
            for i, value in enumerate(pooled):
                pf[i * CH : (i + 1) * CH, cols] = value
                pb[i * CH : (i + 1) * CH, cols] = value.astype(BF)
            for cp in out_copies(j, slot, yv_h, yc_h):
                cp.start()
        return carry

    lax.fori_loop(0, wide // TILE // 2, last, 0)
    exchanges[6][0]()

    core_peer = {"dp": me.dp, "rows": me.x * 2 + 1 - me.c}
    chip_peer = {"dp": me.dp, "rows": (1 - me.x) * 2 + me.c}
    pool_core = remote(pb, pr.at[0], pool_s.at[0], pool_r.at[0], core_peer)
    pool_core.start()
    exchanges[6][1]()
    merge_grads(bx3, tot3)

    def coefs(mi, tot, gn, cols):
        out = []
        for g in (0, 1):
            mean, inv = mi[2 * g : 2 * g + 1, cols], mi[2 * g + 1 : 2 * g + 2, cols]
            dg, ds = tot[2 * g : 2 * g + 1, cols], tot[2 * g + 1 : 2 * g + 2, cols]
            out.append((mean, inv, gn * inv, ds / count[g], dg / count[g]))
        return out

    def grad_three(j, carry):
        cols = lanes(j)
        co = coefs(mi3, tot3, gain(p3, 4, cols), cols)
        for s, g in chunks:
            rows = slice(s, s + CH)
            mean, inv, k0, k1, k2 = co[g]
            nh = (a3[rows, cols] - mean) * inv
            cot[rows, cols] = (k0 * (gpre[rows, cols] - k1 - nh * k2) * mask[rows, 0:1]).astype(BF)
        gwe[:, :, :, :, :, cols] = (
            dot(h2t[...], cot[:, cols]).astype(BF).reshape(gwe.shape[:5] + (TILE,))
        )
        return carry

    lax.fori_loop(0, wide // TILE, grad_three, 0)

    def reducer(k, view, fc, f3, f2, fz):
        return Reduce(me, view, fc, f3, f2, fz, rs_s.at[k], rs_r.at[k])

    q_we = reducer(
        0,
        lambda z, y, x, c, h: gwe.at[z, y, x, c, :, half(h, wide)],
        lambda z, y, x, h: fc_we.at[z, y, x, :, half(h, wide)],
        lambda h: f3_we.at[h],
        lambda h: f2_we.at[h],
        lambda k: fz_we.at[k],
    )
    q_ws = [
        reducer(
            1 + i,
            lambda z, y, x, c, h, i=i: gws.at[3 * i : 3 * i + 3, z, y, x, c, :, half(h, mid)],
            lambda z, y, x, h, i=i: fc_ws.at[3 * i : 3 * i + 3, z, y, x, :, half(h, mid)],
            lambda h, i=i: f3_ws.at[h, 3 * i : 3 * i + 3],
            lambda h, i=i: f2_ws.at[h, 3 * i : 3 * i + 3],
            lambda k, i=i: fz_ws.at[k, 3 * i : 3 * i + 3],
        )
        for i in range(3)
    ]
    q_wr = reducer(
        4,
        lambda z, y, x, c, h: gwr.at[z, y, x, c, :, half(h, mid)],
        lambda z, y, x, h: fc_wr.at[z, y, x, :, half(h, mid)],
        lambda h: f3_wr.at[h],
        lambda h: f2_wr.at[h],
        lambda k: fz_wr.at[k],
    )
    q_we.start()

    def grad_act(gh, a, mi, i, buf, j):
        cols = lanes(j)
        gn, sh = gain(p1, i, cols), gain(p1, i + 1, cols)
        sums = [jnp.zeros((8, TILE), F32) for _ in range(4)]
        for s, g in chunks:
            rows = slice(s, s + CH)
            mean, inv = mi[2 * g : 2 * g + 1, cols], mi[2 * g + 1 : 2 * g + 2, cols]
            nh = (a[rows, cols] - mean) * inv
            zed = nh * gn + sh
            sig = sigmoid(zed)
            gz = gh[rows, cols] * mask[rows, 0:1] * (sig * (1.0 + zed * (1.0 - sig)))
            gh[rows, cols] = gz
            sums[2 * g] = sums[2 * g] + fold(gz * nh)
            sums[2 * g + 1] = sums[2 * g + 1] + fold(gz)
        for k in range(4):
            put(buf, j, k, jnp.sum(sums[k], axis=0, keepdims=True))

    for j in range(mid // TILE):
        w = tile_rows(we, j).reshape(TILE, wide)
        gact[j, :, :] = dot_t(cot[...], w)

    class Cols:
        def __getitem__(self, key):
            rows, cols = key
            return gact[self.j, rows, :]

        def __setitem__(self, key, value):
            rows, cols = key
            gact[self.j, rows, :] = value

    ghs = Cols()
    for j in range(mid // TILE):
        ghs.j = j
        grad_act(ghs, a2, mi2, 2, bx2, j)
    exchanges[5][0]()
    q_we.stage2()
    pool_core.wait()
    pf[...] = pf[...] + pr[0].astype(F32)
    pb[...] = pf[...].astype(BF)
    pool_chip = remote(pb, pr.at[1], pool_s.at[1], pool_r.at[1], chip_peer)
    pool_chip.start()
    exchanges[5][1]()
    merge_grads(bx2, tot2)

    def grad_norm_all(a, mi, tot, i, store):
        for j in range(mid // TILE):
            ghs.j = j
            cols = lanes(j)
            co = coefs(mi, tot, gain(p1, i, cols), cols)
            for s, g in chunks:
                rows = slice(s, s + CH)
                mean, inv, k0, k1, k2 = co[g]
                nh = (a[rows, cols] - mean) * inv
                value = k0 * (ghs[rows, cols] - k1 - nh * k2) * mask[rows, 0:1]
                store(s, cols, value.astype(BF))

    grad_norm_all(a2, mi2, tot2, 2, lambda s, cols, value: store_rows(dv, dc, s, cols, value))
    rim_d[0]()

    def grad_taps(dy):
        def body(dx, carry):
            tap = 3 * dy + dx
            total = dot_r(
                hc[dy, pl.ds(pl.multiple_of(dx * maps_c, maps_c), row_c), :],
                dc[1, maps_c : maps_c + row_c],
            )
            for r in (0, 1):
                total = total + dot_r(
                    hv[r + dy, pl.ds(pl.multiple_of(dx * maps_v, maps_v), row_v), :],
                    dv[1 + r, maps_v : maps_v + row_v],
                )
            gws[tap] = total.astype(BF).reshape(gws.shape[1:])
            return carry

        lax.fori_loop(0, 3, body, 0)

    grad_taps(0)
    q_ws[0].start()
    q_we.stage3()
    grad_taps(1)
    q_ws[1].start()
    q_ws[0].stage2()
    grad_taps(2)
    q_ws[2].start()
    q_ws[1].stage2()
    rim_d[1]()

    gact[...] = jnp.zeros(gact.shape, F32)

    def conv2_back(tap, carry):
        dy, dx = 2 - tap // 3, 2 - tap % 3
        for j in range(mid // TILE):
            w = tile_rows(ws.at[tap], j).reshape(TILE, mid)
            for r in (0, 1):
                left = dv[r + dy, pl.ds(pl.multiple_of(dx * maps_v, maps_v), row_v), :]
                block = gact.at[j, r * row_v : (r + 1) * row_v]
                block[...] = block[...] + dot_t(left, w)
            left = dc[dy, pl.ds(pl.multiple_of(dx * maps_c, maps_c), row_c), :]
            block = gact.at[j, pix_v:pix]
            block[...] = block[...] + dot_t(left, w)
        return carry

    lax.fori_loop(0, 9, conv2_back, 0)
    for j in range(mid // TILE):
        ghs.j = j
        grad_act(ghs, a1, mi1, 0, bx1, j)
    exchanges[4][0]()
    q_we.stage4()
    q_ws[0].stage3()
    q_ws[2].stage2()
    exchanges[4][1]()
    merge_grads(bx1, tot1)

    def store_ga1(s, cols, value):
        ga1[s : s + CH, cols] = value

    grad_norm_all(a1, mi1, tot1, 0, store_ga1)
    for t in range(wide // TILE):
        block = dot(xt[t * TILE : (t + 1) * TILE, :], ga1[...]).astype(BF)
        gwr[t // 2, t % 2] = block.reshape(gwr.shape[2:])
    q_wr.start()
    q_ws[1].stage3()
    q_ws[0].stage4()

    n_dev = n_dp * n_rows

    def three(v):
        hi = v.astype(BF)
        rest = v - hi.astype(F32)
        mid_part = rest.astype(BF)
        return hi, mid_part, (rest - mid_part.astype(F32)).astype(BF)

    def owner_blocks(rows, width):
        share = width // n_dev
        step = 512
        total = jnp.zeros((n_dp * 8, 128), F32)
        for t in range(width // step):
            place = lax.broadcasted_iota(jnp.int32, (step, 128), 1)
            lane = lax.broadcasted_iota(jnp.int32, (step, 128), 0) + t * step
            pick = jnp.where(lane % share == place, 1.0, 0.0).astype(BF)
            owner = (lax.broadcasted_iota(jnp.int32, (8, step), 1) + t * step) // share
            vec = rows[:, t * step : (t + 1) * step]
            stack = jnp.concatenate(
                [jnp.where(owner == d * n_rows + me.r, vec, 0.0) for d in range(n_dp)], axis=0
            )
            for part in three(stack):
                total = total + dot(part, pick)
        return total

    small_rows = [t_[0:1] + t_[2:3] if k == 0 else t_[1:2] + t_[3:4] for t_ in (tot1, tot2) for k in (0, 1)]
    wide_rows = [tot3[0:1] + tot3[2:3], tot3[1:2] + tot3[3:4]]
    narrow = jnp.concatenate(small_rows + [jnp.zeros((4, mid), F32)], axis=0)
    broad = jnp.concatenate([jnp.zeros((4, wide), F32)] + wide_rows + [jnp.zeros((2, wide), F32)], axis=0)
    sb[...] = (owner_blocks(narrow, mid) + owner_blocks(broad, wide)).reshape(sb.shape)

    def small_cp(d, recv):
        peer = (me.dp + n_dp - d) % n_dp if recv else (me.dp + d) % n_dp
        return remote(sb.at[peer], rb.at[d - 1], sm_s.at[d - 1], sm_r.at[d - 1], {"dp": peer, "rows": me.r})

    for d in range(1, n_dp):
        small_cp(d, False).start()

    def grad_in(j):
        cols, slot = lanes(j), j % 2
        previous = (j - 2, gv_h, gc_h) if j >= 2 else (wide // TILE - 2 + j, yv_h, yc_h)
        for cp in out_copies(previous[0], slot, previous[1], previous[2]):
            cp.wait()
        w = wr[j // 2, j % 2].reshape(TILE, mid)
        gpre[:, cols] = gpre[:, cols] + dot_t(ga1[...], w)
        for s, g in chunks:
            store_out(slot, s, gpre[s : s + CH, cols])
        for cp in out_copies(j, slot, gv_h, gc_h):
            cp.start()

    steps = [
        q_wr.stage2, q_ws[2].stage3, q_ws[1].stage4, q_wr.stage3, q_ws[2].stage4, q_wr.stage4,
    ]
    for j in range(wide // TILE):
        grad_in(j)
        if j < 3:
            steps[j]()
    gwe_o[...] = q_we.finish()
    gws_o[0:3] = q_ws[0].finish()
    pool_chip.wait()
    for out, at, maps, valid in ((poolv_o, 0, maps_v, valid_v), (poolc_o, maps_v, maps_c, valid_c)):
        total = pf[at : at + maps] + pr[1, at : at + maps].astype(F32)
        out[...] = (total * (1.0 / valid)).reshape(out.shape)
    for step in steps[3:]:
        step()
    total = sb[me.dp]
    for d in range(1, n_dp):
        small_cp(d, True).wait_recv()
        total = total + rb[d - 1]
    small_o[...] = total
    gws_o[3:6] = q_ws[1].finish()
    gws_o[6:9] = q_ws[2].finish()
    gwr_o[...] = q_wr.finish()

    for j in (wide // TILE - 2, wide // TILE - 1):
        for cp in out_copies(j, j % 2, gv_h, gc_h):
            cp.wait()
    small_piece.drain()
    for p in pieces:
        p.drain()
    for e in exchanges:
        e[2]()
    rim_h[2]()
    rim_d[2]()
    for q in [q_we] + q_ws + [q_wr]:
        q.drain()
    for d in range(1, n_dp):
        small_cp(d, False).wait_send()


def block_step(n_dp, n_rows, xv, xc, mv, mc, wr, ws, we, g1, s1, g2, s2, g3, s3, cv, cc, cpv, cpc):
    img, views, rows_v, cols_v, wide = xv.shape
    crops, cols_c = xc.shape[1], xc.shape[3]
    mid = wr.shape[1]
    maps_v, maps_c = img * views, img * crops
    pix_v, pix_c = rows_v * cols_v * maps_v, cols_c * maps_c
    pix = pix_v + pix_c
    valid_v, valid_c = (rows_v * n_rows - 1) * cols_v, (n_rows - 1) * cols_c
    nz, nx = n_dp // 2, n_rows // 2

    def views_in(t):
        return t.transpose(0, 1, 3, 2, 4).reshape(maps_v, cols_v, rows_v, wide)

    def crops_in(t):
        return t.transpose(0, 2, 3, 1, 4).reshape(img, cols_c, crops, wide)

    grid4 = (nz, 2, nx, 2)
    vm = pl.BlockSpec(memory_space=pltpu.VMEM)
    hbm = pl.BlockSpec(memory_space=pl.ANY)
    s_wr, s_we = wr.shape[0], we.shape[0]
    V = pltpu.VMEM
    D = pltpu.SemaphoreType.DMA

    scratch = [
        V(grid4 + (s_wr, mid), BF), V((9,) + grid4 + (s_we, mid), BF), V(grid4 + (s_we, wide), BF),
        V(grid4 + (8, 128), F32),
        V((pix, 128), F32), V((cols_v, maps_v, 2, wide), BF), V((img, cols_c, crops, wide), BF),
        V((img, views, wide), F32), V((img, crops, wide), F32),
        V((pix, wide), BF), V((wide, pix), BF), V((pix, wide), BF),
        V((pix, mid), F32), V((pix, mid), F32), V((pix, wide), F32), V((pix, wide), F32),
        V((2, maps_v, cols_v, 2, TILE), F32), V((2, maps_c, cols_c, TILE // 128, 128), F32), V((2, pix, TILE), F32),
        V((4, (cols_v + 2) * maps_v, mid), BF), V((3, (cols_c + 2) * maps_c, mid), BF),
        V((4, (cols_v + 2) * maps_v, mid), BF), V((3, (cols_c + 2) * maps_c, mid), BF),
        V((pix, mid), BF), V((mid, pix), BF), V((pix, mid), BF),
        V(grid4 + (s_wr, mid), BF), V((9,) + grid4 + (s_we, mid), BF), V(grid4 + (s_we, wide), BF),
        V((nz, 2, nx, s_we, wide), BF), V((9, nz, 2, nx, s_we, mid), BF), V((nz, 2, nx, s_wr, mid), BF),
        V((2, nz, 2, s_we, wide // 2), BF), V((2, 9, nz, 2, s_we, mid // 2), BF), V((2, nz, 2, s_wr, mid // 2), BF),
        V((2, nz, s_we, wide // 2), BF), V((2, 9, nz, s_we, mid // 2), BF), V((2, nz, s_wr, mid // 2), BF),
        V((nz - 1, s_we, wide), BF), V((nz - 1, 9, s_we, mid), BF), V((nz - 1, s_wr, mid), BF),
        V((8, mid), F32), V((8, wide), F32),
        V((4, mid), F32), V((4, mid), F32), V((4, wide), F32),
        V((n_rows, 8, 128), F32),
        V((n_rows, 8, mid // 2), F32), V((n_rows, 8, mid // 2), F32), V((n_rows, 8, wide // 2), F32),
        V((n_rows, 8, mid // 2), F32), V((n_rows, 8, mid // 2), F32), V((n_rows, 8, wide // 2), F32),
        V((4, mid), F32), V((4, mid), F32), V((4, wide), F32),
        V((maps_v + maps_c, wide), F32), V((maps_v + maps_c, wide), BF), V((2, maps_v + maps_c, wide), BF),
        V((n_dp, 8, 128), F32), V((n_dp - 1, 8, 128), F32),
        D((3, cols_v + 1)), D((2, 2)), D((6, 12)), D((6, 12)), D((5, 5 + nz)), D((5, 5 + nz)),
        D((7, n_rows - 1)), D((7, n_rows - 1)), D((2, 4)), D((2, 4)), D((2,)), D((2,)), D((n_dp - 1,)), D((n_dp - 1,)),
    ]
    out_v = jax.ShapeDtypeStruct((maps_v, cols_v, 2, wide), F32)
    out_c = jax.ShapeDtypeStruct((maps_c, cols_c, wide // TILE, TILE // 128, 128), F32)
    outs = pl.pallas_call(
        functools.partial(kernel, n_dp, n_rows, (maps_v, cols_v, maps_c, cols_c, valid_v, valid_c)),
        out_shape=[
            out_v, out_c, out_v, out_c,
            jax.ShapeDtypeStruct(cpv.shape, F32), jax.ShapeDtypeStruct(cpc.shape, F32),
            jax.ShapeDtypeStruct((s_wr, mid), F32), jax.ShapeDtypeStruct((9, s_we, mid), F32),
            jax.ShapeDtypeStruct((s_we, wide), F32), jax.ShapeDtypeStruct((8, 128), F32),
        ],
        in_specs=[hbm] * 6 + [vm] * 11,
        out_specs=[hbm] * 4 + [vm] * 6,
        scratch_shapes=scratch,
        compiler_params=pltpu.CompilerParams(
            collective_id=0, has_side_effects=True, vmem_limit_bytes=63 << 20
        ),
    )(
        views_in(xv), crops_in(xc), views_in(cv), crops_in(cc), cpv, cpc,
        mv.transpose(1, 2, 0), mc.transpose(1, 2, 0), wr, ws.reshape(9, s_we, mid), we,
        g1.reshape(1, -1), s1.reshape(1, -1), g2.reshape(1, -1), s2.reshape(1, -1),
        g3.reshape(1, -1), s3.reshape(1, -1),
    )
    yv, yc, gv, gc, pool_v, pool_c, gwr, gws, gwe, small = outs

    def views_out(t):
        return t.reshape(img, views, cols_v, rows_v, wide).transpose(0, 1, 3, 2, 4)

    def crops_out(t):
        return t.reshape(img, crops, 1, cols_c, wide)

    e = mid // (n_dp * n_rows)
    f = wide // (n_dp * n_rows)
    return (
        views_out(yv), crops_out(yc),
        pool_v, pool_c,
        views_out(gv), crops_out(gc),
        gwr, gws.reshape(3, 3, s_we, mid), gwe,
        small[0, :e], small[1, :e], small[2, :e], small[3, :e], small[4, :f], small[5, :f],
    )


def fits(xv, xc, we):
    return we.shape[0] % 16 == 0 and xv.shape[2] == 2 and xc.shape[2] == 1


def with_halo(block, sides, width):
    for axis, dim in sides:
        count = lax.axis_size(axis)
        forward = [(i, i + 1) for i in range(count - 1)]
        backward = [(target, source) for source, target in forward]
        low = lax.ppermute(
            lax.slice_in_dim(block, block.shape[dim] - width, None, axis=dim), axis, forward
        )
        high = lax.ppermute(lax.slice_in_dim(block, 0, width, axis=dim), axis, backward)
        block = jnp.concatenate([low, block, high], axis=dim)
    return block


def from_behind(array, axis, by):
    peers = lax.axis_size(axis)
    pairs = [(i, i + by) for i in range(peers) if 0 <= i + by < peers]
    return lax.ppermute(array, axis, pairs)


def silu_slope(value):
    sig = jax.nn.sigmoid(value)
    return sig * (1.0 + value * (1.0 - sig))


def pixel_mask(mask_rows, col_count):
    expanded = jnp.broadcast_to(
        mask_rows.astype(jnp.float32)[..., None], mask_rows.shape + (col_count,)
    )
    return expanded.reshape(-1, 1)


def by_group(in_views, view_value, crop_value):
    return jnp.where(in_views, view_value, crop_value)


def norm_forward(acts, mask_col, view_pixels, in_views, counts, gain_vec, shift_vec):
    masked = acts * mask_col
    totals = lax.psum(
        (jnp.sum(masked[:view_pixels], axis=0), jnp.sum(masked[view_pixels:], axis=0)), "rows"
    )
    centered = acts - by_group(in_views, totals[0] / counts[0], totals[1] / counts[1])
    squares = jnp.square(centered * mask_col)
    spread = lax.psum(
        (jnp.sum(squares[:view_pixels], axis=0), jnp.sum(squares[view_pixels:], axis=0)), "rows"
    )
    inv_rows = by_group(
        in_views, lax.rsqrt(spread[0] / counts[0] + eps), lax.rsqrt(spread[1] / counts[1] + eps)
    )
    normal = centered * inv_rows
    return (normal * gain_vec + shift_vec, normal, inv_rows)


def norm_backward(grad_z, normal, inv_rows, mask_col, view_pixels, in_views, counts, gain_vec):
    product = grad_z * normal
    partials = (
        jnp.sum(product[:view_pixels], axis=0),
        jnp.sum(grad_z[:view_pixels], axis=0),
        jnp.sum(product[view_pixels:], axis=0),
        jnp.sum(grad_z[view_pixels:], axis=0),
    )
    totals = (
        lax.psum(partials[0].astype(jnp.bfloat16), "rows").astype(jnp.float32),
        lax.psum(partials[1].astype(jnp.bfloat16), "rows").astype(jnp.float32),
        lax.psum(partials[2].astype(jnp.bfloat16), "rows").astype(jnp.float32),
        lax.psum(partials[3].astype(jnp.bfloat16), "rows").astype(jnp.float32),
    )
    scale_mean = by_group(in_views, totals[0] / counts[0], totals[2] / counts[1])
    shift_mean = by_group(in_views, totals[1] / counts[0], totals[3] / counts[1])
    grad_acts = gain_vec * inv_rows * (grad_z - shift_mean - normal * scale_mean) * mask_col
    return (grad_acts.astype(jnp.bfloat16), partials[0] + partials[2], partials[1] + partials[3])


def with_rims(feature_map):
    extended = with_halo(feature_map, (("rows", 1),), 1)
    return jnp.pad(extended, ((0, 0), (0, 0), (1, 1), (0, 0)))


def gather_taps(extended, row_count, col_count):
    windows = []
    for row_step in range(3):
        for col_step in range(3):
            windows.append(
                extended[:, row_step : row_step + row_count, col_step : col_step + col_count, :]
            )
    return jnp.concatenate(windows, axis=-1).reshape(-1, 9 * extended.shape[-1])


def spread_taps(grad_patches, map_count, row_count, col_count, mid_width):
    pieces = grad_patches.reshape(map_count, row_count, col_count, 9, mid_width)
    padded = jnp.zeros((map_count, row_count + 2, col_count + 2, mid_width), jnp.float32)
    tap_index = 0
    for row_step in range(3):
        for col_step in range(3):
            padded = padded.at[
                :, row_step : row_step + row_count, col_step : col_step + col_count, :
            ].add(pieces[:, :, :, tap_index, :])
            tap_index += 1
    inside = padded[:, 1 : row_count + 1, 1 : col_count + 1, :]
    from_below = from_behind(
        padded[:, 0, 1 : col_count + 1, :].astype(jnp.bfloat16), "rows", -1
    ).astype(jnp.float32)
    from_above = from_behind(
        padded[:, row_count + 1, 1 : col_count + 1, :].astype(jnp.bfloat16), "rows", 1
    ).astype(jnp.float32)
    inside = inside.at[:, row_count - 1].add(from_below)
    inside = inside.at[:, 0].add(from_above)
    return inside.reshape(-1, mid_width)


def contract_rows(left, right):
    return lax.dot_general(
        left, right, (((0,), (0,)), ((), ())), preferred_element_type=jnp.float32
    )


def contract_cols(left, right):
    return lax.dot_general(
        left, right, (((1,), (1,)), ((), ())), preferred_element_type=jnp.float32
    )


def shards(
    x_views,
    x_crops,
    mask_views,
    mask_crops,
    w_reduce,
    w_spatial,
    w_expand,
    gain_reduce,
    shift_reduce,
    gain_spatial,
    shift_spatial,
    gain_expand,
    shift_expand,
    cot_views,
    cot_crops,
    cot_pool_views,
    cot_pool_crops,
):
    low_type = jnp.bfloat16
    gathered = (
        lax.all_gather(w_reduce.astype(low_type), ("dp", "rows"), axis=0, tiled=True),
        lax.all_gather(w_spatial.astype(low_type), ("dp", "rows"), axis=2, tiled=True),
        lax.all_gather(w_expand.astype(low_type), ("dp", "rows"), axis=0, tiled=True),
        lax.all_gather(gain_reduce.astype(low_type), ("dp", "rows"), axis=0, tiled=True),
        lax.all_gather(shift_reduce.astype(low_type), ("dp", "rows"), axis=0, tiled=True),
        lax.all_gather(gain_spatial.astype(low_type), ("dp", "rows"), axis=0, tiled=True),
        lax.all_gather(shift_spatial.astype(low_type), ("dp", "rows"), axis=0, tiled=True),
        lax.all_gather(gain_expand.astype(low_type), ("dp", "rows"), axis=0, tiled=True),
        lax.all_gather(shift_expand.astype(low_type), ("dp", "rows"), axis=0, tiled=True),
    )
    weight_one, weight_two, weight_three = (gathered[0], gathered[1], gathered[2])
    gain_one, shift_one, gain_two, shift_two, gain_three, shift_three = [
        entry.astype(jnp.float32) for entry in gathered[3:]
    ]
    in_width = weight_one.shape[0]
    mid_width = weight_one.shape[1]
    view_maps = x_views.shape[0] * x_views.shape[1]
    view_rows, view_cols = (x_views.shape[2], x_views.shape[3])
    crop_maps = x_crops.shape[0] * x_crops.shape[1]
    crop_rows, crop_cols = (x_crops.shape[2], x_crops.shape[3])
    view_pixels = view_maps * view_rows * view_cols
    total_pixels = view_pixels + crop_maps * crop_rows * crop_cols
    row_parts = lax.axis_size("rows")
    view_valid = (view_rows * row_parts - 1) * view_cols
    crop_valid = (crop_rows * row_parts - 1) * crop_cols
    counts = (float(view_maps * view_valid), float(crop_maps * crop_valid))
    mask_col = jnp.concatenate(
        [pixel_mask(mask_views, view_cols), pixel_mask(mask_crops, crop_cols)], axis=0
    )
    in_views = lax.broadcasted_iota(jnp.int32, (total_pixels, 1), 0) < view_pixels
    inputs = jnp.concatenate([x_views.reshape(-1, in_width), x_crops.reshape(-1, in_width)], axis=0)
    acts_one = jnp.dot(inputs, weight_one, preferred_element_type=jnp.float32)
    z_one, normal_one, inv_one = norm_forward(
        acts_one, mask_col, view_pixels, in_views, counts, gain_one, shift_one
    )
    hidden_one = (jax.nn.silu(z_one) * mask_col).astype(low_type)
    view_hidden = hidden_one[:view_pixels].reshape(view_maps, view_rows, view_cols, mid_width)
    crop_hidden = hidden_one[view_pixels:].reshape(crop_maps, crop_rows, crop_cols, mid_width)
    patches = jnp.concatenate(
        [
            gather_taps(with_rims(view_hidden), view_rows, view_cols),
            gather_taps(with_rims(crop_hidden), crop_rows, crop_cols),
        ],
        axis=0,
    )
    spatial_flat = weight_two.reshape(9 * mid_width, mid_width)
    acts_two = jnp.dot(patches, spatial_flat, preferred_element_type=jnp.float32)
    z_two, normal_two, inv_two = norm_forward(
        acts_two, mask_col, view_pixels, in_views, counts, gain_two, shift_two
    )
    hidden_two = (jax.nn.silu(z_two) * mask_col).astype(low_type)
    acts_three = jnp.dot(hidden_two, weight_three, preferred_element_type=jnp.float32)
    z_three, normal_three, inv_three = norm_forward(
        acts_three, mask_col, view_pixels, in_views, counts, gain_three, shift_three
    )
    pre_act = inputs.astype(jnp.float32) + z_three
    result = jax.nn.silu(pre_act) * mask_col
    pooled = (
        lax.psum(
            jnp.sum(
                result[:view_pixels].reshape(view_maps, view_rows * view_cols, in_width), axis=1
            ).astype(jnp.bfloat16),
            "rows",
        ).astype(jnp.float32),
        lax.psum(
            jnp.sum(
                result[view_pixels:].reshape(crop_maps, crop_rows * crop_cols, in_width), axis=1
            ).astype(jnp.bfloat16),
            "rows",
        ).astype(jnp.float32),
    )
    pool_views = (pooled[0] / view_valid).reshape(cot_pool_views.shape)
    pool_crops = (pooled[1] / crop_valid).reshape(cot_pool_crops.shape)
    view_grad = (
        cot_views.astype(jnp.float32).reshape(view_maps, view_rows * view_cols, in_width)
        + cot_pool_views.reshape(view_maps, 1, in_width) / view_valid
    )
    crop_grad = (
        cot_crops.astype(jnp.float32).reshape(crop_maps, crop_rows * crop_cols, in_width)
        + cot_pool_crops.reshape(crop_maps, 1, in_width) / crop_valid
    )
    grad_out = jnp.concatenate(
        [view_grad.reshape(-1, in_width), crop_grad.reshape(-1, in_width)], axis=0
    )
    grad_pre = grad_out * mask_col * silu_slope(pre_act)
    grad_three, dgain_three, dshift_three = norm_backward(
        grad_pre, normal_three, inv_three, mask_col, view_pixels, in_views, counts, gain_three
    )
    grad_expand = contract_rows(hidden_two, grad_three)
    grad_hidden_two = contract_cols(grad_three, weight_three)
    grad_z_two = grad_hidden_two * mask_col * silu_slope(z_two)
    grad_two, dgain_two, dshift_two = norm_backward(
        grad_z_two, normal_two, inv_two, mask_col, view_pixels, in_views, counts, gain_two
    )
    grad_spatial = contract_rows(patches, grad_two).reshape(3, 3, mid_width, mid_width)
    grad_patches = contract_cols(grad_two, spatial_flat)
    grad_hidden_one = jnp.concatenate(
        [
            spread_taps(grad_patches[:view_pixels], view_maps, view_rows, view_cols, mid_width),
            spread_taps(grad_patches[view_pixels:], crop_maps, crop_rows, crop_cols, mid_width),
        ],
        axis=0,
    )
    grad_z_one = grad_hidden_one * mask_col * silu_slope(z_one)
    grad_one, dgain_one, dshift_one = norm_backward(
        grad_z_one, normal_one, inv_one, mask_col, view_pixels, in_views, counts, gain_one
    )
    grad_reduce = contract_rows(inputs, grad_one)
    grad_inputs = contract_cols(grad_one, weight_one) + grad_pre
    summed = (
        lax.psum_scatter(grad_reduce, ("dp", "rows"), scatter_dimension=0, tiled=True),
        lax.psum_scatter(grad_spatial, ("dp", "rows"), scatter_dimension=2, tiled=True),
        lax.psum_scatter(grad_expand, ("dp", "rows"), scatter_dimension=0, tiled=True),
        lax.psum_scatter(dgain_one, ("dp", "rows"), scatter_dimension=0, tiled=True),
        lax.psum_scatter(dshift_one, ("dp", "rows"), scatter_dimension=0, tiled=True),
        lax.psum_scatter(dgain_two, ("dp", "rows"), scatter_dimension=0, tiled=True),
        lax.psum_scatter(dshift_two, ("dp", "rows"), scatter_dimension=0, tiled=True),
        lax.psum_scatter(dgain_three, ("dp", "rows"), scatter_dimension=0, tiled=True),
        lax.psum_scatter(dshift_three, ("dp", "rows"), scatter_dimension=0, tiled=True),
    )
    out_views = result[:view_pixels].reshape(x_views.shape)
    out_crops = result[view_pixels:].reshape(x_crops.shape)
    grad_views = grad_inputs[:view_pixels].reshape(x_views.shape)
    grad_crops = grad_inputs[view_pixels:].reshape(x_crops.shape)
    return (
        out_views,
        out_crops,
        pool_views,
        pool_crops,
        grad_views,
        grad_crops,
        summed[0],
        summed[1],
        summed[2],
        summed[3],
        summed[4],
        summed[5],
        summed[6],
        summed[7],
        summed[8],
    )


def solution(mesh):
    in_specs = (
        P("dp", None, "rows", None, None),
        P("dp", None, "rows", None, None),
        P("dp", None, "rows"),
        P("dp", None, "rows"),
        P(("dp", "rows"), None),
        P(None, None, ("dp", "rows"), None),
        P(("dp", "rows"), None),
        P(("dp", "rows")),
        P(("dp", "rows")),
        P(("dp", "rows")),
        P(("dp", "rows")),
        P(("dp", "rows")),
        P(("dp", "rows")),
        P("dp", None, "rows", None, None),
        P("dp", None, "rows", None, None),
        P("dp", None, None),
        P("dp", None, None),
    )
    out_specs = (
        P("dp", None, "rows", None, None),
        P("dp", None, "rows", None, None),
        P("dp", None, None),
        P("dp", None, None),
        P("dp", None, "rows", None, None),
        P("dp", None, "rows", None, None),
        P(("dp", "rows"), None),
        P(None, None, ("dp", "rows"), None),
        P(("dp", "rows"), None),
        P(("dp", "rows")),
        P(("dp", "rows")),
        P(("dp", "rows")),
        P(("dp", "rows")),
        P(("dp", "rows")),
        P(("dp", "rows")),
    )
    def step(*args):
        if fits(args[0], args[1], args[6]):
            return block_step(mesh.shape["dp"], mesh.shape["rows"], *args)
        return shards(*args)

    return jax.shard_map(step, mesh=mesh, in_specs=in_specs, out_specs=out_specs, check_vma=False)
```

profile of v0, /device:TPU:0, one launch (start us, length us, event | category | flops | bytes accessed | tf_op | source)
XLA Modules:
  0.0 173.8 jit_solution(14542180722330559516)
XLA Ops:
  0.7 155.5 %shard_map.280 = (f32[32,7,2,2048]{3,2,1,0:T(2,128)}, f32[64,3,8,2,128]{4,3,2,1,0:T(2,128)}, f32[32,7,2,2048]{3,2,1,0:T(2,128)}, f32[64,3,8,2,128]{4,3,2,1,0:T(2...) custom-call(bf16[32,7,2,2048]{3,2,1,0:T(2,128)(2,1)} %bitcast.48, ...), custom_call_target="tpu_custom_call" | custom-call | tf_op jit(solution)/shard_map/pallas_call | solution.py:1030
  156.2 1.3 slice_bitcast_fusion.2
  157.5 1.3 slice_bitcast_fusion
  158.8 0.0 copy-start.2
  158.8 0.0 copy-start.5
  158.8 0.0 copy-start.3
  158.8 6.6 %copy.55 = f32[16,2,2,7,2048]{4,2,3,1,0:T(2,128)} copy(f32[16,2,2,7,2048]{4,2,3,1,0:T(2,128)} %bitcast.47) | data formatting | bytes 7340032
  165.4 0.0 copy-done.2
  165.4 0.0 copy-start
  165.4 1.1 copy.56
  166.5 0.0 copy-done.5
  166.6 0.7 copy.57
  167.3 0.0 copy-done.3
  167.3 0.8 copy.58
  168.1 0.1 copy-done
  168.1 1.8 %copy.59 = f32[16,2,2,7,2048]{4,2,3,1,0:T(2,128)} copy(f32[16,2,2,7,2048]{4,2,3,1,0:T(2,128)S(1)} %bitcast.46) | data formatting | bytes 7340032
  169.9 0.7 copy-done.1
  170.7 1.1 copy.60
  171.8 0.0 copy-done.7
  171.8 0.7 copy.61
  172.5 0.0 copy-done.4
  172.5 0.7 copy.62
  173.2 0.0 copy-done.6
  173.2 0.7 copy.63
  (4 shorter events, 0.0 us)
Async XLA Ops:
  158.8 6.6 %copy-start.2 = (f32[64,3,8,2,128]{4,3,2,1,0:T(2,128)S(1)}, f32[64,3,8,2,128]{4,3,2,1,0:T(2,128)}, u32[]{:S(2)}) copy-start(f32[64,3,8,2,128]{4,3,2,1,0:T(2,128)} %get-tuple-element.26) | copy-start | bytes 4718596
  158.8 7.8 %copy-start.5 = (f32[16,2,2048]{2,1,0:T(2,128)S(1)}, f32[16,2,2048]{2,1,0:T(2,128)}, u32[]{:S(2)}) copy-start(f32[16,2,2048]{2,1,0:T(2,128)} %get-tuple-element.88) | copy-start | bytes 786436
  158.8 8.5 %copy-start.3 = (f32[16,4,2048]{2,1,0:T(4,128)S(1)}, f32[16,4,2048]{2,1,0:T(4,128)}, u32[]{:S(2)}) copy-start(f32[16,4,2048]{2,1,0:T(4,128)} %get-tuple-element.89) | copy-start | bytes 1572868
  165.4 2.7 %copy-start = (f32[32,7,2,2048]{3,2,1,0:T(2,128)S(1)}, f32[32,7,2,2048]{3,2,1,0:T(2,128)}, u32[]{:S(2)}) copy-start(f32[32,7,2,2048]{3,2,1,0:T(2,128)} %get-tuple-element.29) | copy-start | bytes 11010052
  168.1 2.5 %copy-start.1 = (f32[64,3,8,2,128]{4,3,2,1,0:T(2,128)S(1)}, f32[64,3,8,2,128]{4,3,2,1,0:T(2,128)}, u32[]{:S(2)}) copy-start(f32[64,3,8,2,128]{4,3,2,1,0:T(2,128)} %get-tuple-element.30) | copy-start | bytes 4718596
  170.7 1.2 copy-start.7
  170.7 1.8 %copy-start.4 = (f32[9,16,512]{2,1,0:T(8,128)S(1)}, f32[9,16,512]{2,1,0:T(8,128)}, u32[]{:S(2)}) copy-start(f32[9,16,512]{2,1,0:T(8,128)} %get-tuple-element.32) | copy-start | bytes 884740
  170.7 2.5 %copy-start.6 = (f32[16,2048]{1,0:T(8,128)S(1)}, f32[16,2048]{1,0:T(8,128)}, u32[]{:S(2)}) copy-start(f32[16,2048]{1,0:T(8,128)} %get-tuple-element.94) | copy-start | bytes 393220
where the time goes:
time: 174 us
  Pallas kernels  156 us (90%)
  local copies, waits for them, and re-layouts  17.7 us (10%)
    pallas_call x1, Pallas kernels, block_step(): pl.pallas_call(functools.partial(kernel, n_dp, n_rows, (maps_v, cols_v, m...  156 us
    unnamed x25, local copies, waits for them, and re-layouts  15 us

commit v1 on v0

--- a/solution.py
+++ b/solution.py
@@ -21,8 +21,10 @@
     return pl.ds(pl.multiple_of(j * width, width), width)
 
 
-def half(h, width):
-    return ALL if h is None else slice(h * (width // 2), (h + 1) * (width // 2))
+def half(h, width, at=0, whole=None):
+    if h is None:
+        return ALL if whole is None else slice(at, at + whole)
+    return slice(at + h * (width // 2), at + (h + 1) * (width // 2))
 
 
 def dot(a, b):
@@ -60,89 +62,173 @@
     )
 
 
-class Gather:
+class Piece:
+    def __init__(self, me, view, ssem, rsem):
+        self.me, self.view, self.s, self.r, self.sent = me, view, ssem, rsem, []
+        self.px = me.dev(me.z, me.y, 1 - me.x, me.c)
+        self.py = me.dev(me.z, 1 - me.y, me.x, me.c)
+        self.pc = me.dev(me.z, me.y, me.x, 1 - me.c)
+
+    def pz(self, k):
+        return self.me.dev((self.me.z + k) % self.me.nz, self.me.y, self.me.x, self.me.c)
+
+    def send(self, k, src, dst, to):
+        cp = remote(src, dst, self.s.at[k], self.r.at[k], to)
+        cp.start()
+        self.sent.append(cp)
+
+    def got(self, k, dst):
+        remote(dst, dst, self.s.at[k], self.r.at[k], self.pc).wait_recv()
+
+    def drain(self):
+        for cp in self.sent:
+            cp.wait_send()
+
+
+class Gather(Piece):
     def __init__(self, me, view, ssem, rsem, halves=(0, 1)):
-        self.me, self.view, self.s, self.r, self.halves = me, view, ssem, rsem, halves
-
-    def cp(self, k, place, to):
-        ref = self.view(*place)
-        return remote(ref, ref, self.s.at[k], self.r.at[k], self.me.dev(*to))
-
-    def along_z(self, dz, recv):
-        me = self.me
-        if recv:
-            z = (me.z + me.nz - dz) % me.nz
-            return self.cp(dz - 1, (z, me.y, me.x, me.c, None), (z, me.y, me.x, me.c))
-        to = ((me.z + dz) % me.nz, me.y, me.x, me.c)
-        return self.cp(dz - 1, (me.z, me.y, me.x, me.c, None), to)
-
-    def second(self, h, recv):
-        me = self.me
-        yy, xx = (1 - me.y, me.x) if h == 0 else (me.y, 1 - me.x)
-        place = (ALL, yy, xx, me.c, h) if recv else (ALL, me.y, me.x, me.c, h)
-        return self.cp(3 + h, place, (me.z, yy, xx, me.c))
-
-    def third(self, h, recv):
-        me = self.me
-        if h == 0:
-            return self.cp(
-                5, (ALL, ALL, 1 - me.x if recv else me.x, me.c, h), (me.z, me.y, 1 - me.x, me.c)
-            )
-        return self.cp(
-            6, (ALL, 1 - me.y if recv else me.y, ALL, me.c, h), (me.z, 1 - me.y, me.x, me.c)
-        )
-
-    def core(self, k, recv):
-        me = self.me
-        c = 1 - me.c if recv else me.c
-        place = (
-            (ALL, me.y, me.x, c, None),
-            (ALL, 1 - me.y, me.x, c, 0),
-            (ALL, me.y, 1 - me.x, c, 1),
-            (ALL, ALL, 1 - me.x, c, 0),
-            (ALL, 1 - me.y, ALL, c, 1),
-        )[k]
-        return self.cp(7 + k, place, (me.z, me.y, me.x, 1 - me.c))
-
+        super().__init__(me, view, ssem, rsem)
+        self.halves, n = halves, me.nz
+        self.X, self.Y, self.D, self.C = n - 1, 2 * n - 1, (3 * n - 1, 4 * n - 1), 5 * n - 1
+
+    def share(self, k, z, y, x, h, to):
+        ref = self.view(z, y, x, self.me.c, h)
+        self.send(k, ref, ref, to)
+
+    def wait(self, k, z, y, x, h, c=None):
+        self.got(k, self.view(z, y, x, self.me.c if c is None else c, h))
+
+    def source(self, k):
+        return (self.me.z + self.me.nz - k) % self.me.nz
+
+    def start_z(self):
+        me = self.me
+        for k in range(1, me.nz):
+            self.share(k - 1, me.z, me.y, me.x, None, self.pz(k))
+
+    def start_xy(self):
+        me = self.me
+        self.share(self.X, me.z, me.y, me.x, None, self.px)
+        self.share(self.Y, me.z, me.y, me.x, None, self.py)
+
+    def got_z(self, k):
+        me, z = self.me, self.source(k)
+        self.wait(k - 1, z, me.y, me.x, None)
+        self.share(self.X + k, z, me.y, me.x, None, self.px)
+        self.share(self.Y + k, z, me.y, me.x, None, self.py)
+        if k == me.nz - 1:
+            self.share(self.C, ALL, me.y, me.x, None, self.pc)
+
+    def diagonal(self):
+        me = self.me
+        for k in range(me.nz):
+            z = self.source(k)
+            self.wait(self.Y + k, z, 1 - me.y, me.x, None)
+            self.share(self.D[0] + k, z, 1 - me.y, me.x, 0, self.px)
+            self.wait(self.X + k, z, me.y, 1 - me.x, None)
+            if 1 in self.halves:
+                self.share(self.D[1] + k, z, me.y, 1 - me.x, 1, self.py)
+        self.share(self.C + 1, ALL, 1 - me.y, me.x, None, self.pc)
+        self.share(self.C + 2, ALL, me.y, 1 - me.x, None, self.pc)
+
+    def last(self):
+        me = self.me
+        for h in self.halves:
+            for k in range(me.nz):
+                self.wait(self.D[h] + k, self.source(k), 1 - me.y, 1 - me.x, h)
+            self.share(self.C + 3 + h, ALL, 1 - me.y, 1 - me.x, h, self.pc)
+
+    def finish(self):
+        me, o = self.me, 1 - self.me.c
+        self.wait(self.C, ALL, me.y, me.x, None, o)
+        self.wait(self.C + 1, ALL, 1 - me.y, me.x, None, o)
+        self.wait(self.C + 2, ALL, me.y, 1 - me.x, None, o)
+        for h in self.halves:
+            self.wait(self.C + 3 + h, ALL, 1 - me.y, 1 - me.x, h, o)
+
+
+class GatherPlane(Gather):
     def start(self):
-        for dz in range(1, self.me.nz):
-            self.along_z(dz, False).start()
-
-    def got_z(self):
-        for dz in range(1, self.me.nz):
-            self.along_z(dz, True).wait_recv()
+        me = self.me
+        self.share(0, me.z, me.y, me.x, None, self.px)
+        self.share(1, me.z, me.y, me.x, None, self.py)
+
+    def diagonal(self):
+        me = self.me
+        self.wait(1, me.z, 1 - me.y, me.x, None)
+        self.share(2, me.z, 1 - me.y, me.x, 0, self.px)
+        self.wait(0, me.z, me.y, 1 - me.x, None)
+        self.share(3, me.z, me.y, 1 - me.x, 1, self.py)
+
+    def plane(self):
+        me = self.me
+        for h in (0, 1):
+            self.wait(2 + h, me.z, 1 - me.y, 1 - me.x, h)
+        for k in range(1, me.nz):
+            self.share(3 + k, me.z, ALL, ALL, None, self.pz(k))
+        self.share(4 + me.nz, me.z, ALL, ALL, None, self.pc)
+
+    def last(self):
+        for k in range(1, self.me.nz):
+            self.wait(3 + k, self.source(k), ALL, ALL, None)
+            self.share(4 + self.me.nz + k, self.source(k), ALL, ALL, None, self.pc)
+
+    def finish(self):
+        for k in range(self.me.nz):
+            self.wait(4 + self.me.nz + k, self.source(k), ALL, ALL, None, 1 - self.me.c)
+
+
+class ReducePlane(Piece):
+    def __init__(self, me, view, from_core, from_z, from_diagonal, from_xy, ssem, rsem):
+        super().__init__(me, view, ssem, rsem)
+        self.fc, self.fz, self.fd, self.fxy = from_core, from_z, from_diagonal, from_xy
+        self.DG, self.H = me.nz, me.nz + 2
+
+    def start(self):
+        c = self.me.c
+        self.send(0, self.view(ALL, ALL, ALL, 1 - c, None), self.fc(), self.pc)
 
     def stage2(self):
-        for h in self.halves:
-            self.second(h, False).start()
-        self.core(0, False).start()
+        me = self.me
+        self.got(0, self.fc())
+        ref = self.view(ALL, ALL, ALL, me.c, None)
+        ref[...] = ref[...] + self.fc()[...]
+        for k in range(1, me.nz):
+            z = (me.z + k) % me.nz
+            self.send(k, self.view(z, ALL, ALL, me.c, None), self.fz(k - 1), self.pz(k))
 
     def stage3(self):
-        for h in self.halves:
-            self.second(h, True).wait_recv()
-            self.third(h, False).start()
-            self.core(1 + h, False).start()
+        me = self.me
+        ref = self.view(me.z, ALL, ALL, me.c, None)
+        total = ref[...].astype(F32)
+        for k in range(1, me.nz):
+            self.got(k, self.fz(k - 1))
+            total = total + self.fz(k - 1)[...].astype(F32)
+        ref[...] = total.astype(BF)
+        self.send(self.DG, self.view(me.z, 1 - me.y, 1 - me.x, me.c, 0), self.fd(0), self.px)
+        self.send(self.DG + 1, self.view(me.z, 1 - me.y, 1 - me.x, me.c, 1), self.fd(1), self.py)
+        self.send(self.H, self.view(me.z, me.y, 1 - me.x, me.c, 0), self.fxy(0, 0), self.px)
+        self.send(self.H + 1, self.view(me.z, 1 - me.y, me.x, me.c, 1), self.fxy(1, 1), self.py)
 
     def stage4(self):
-        for h in self.halves:
-            self.third(h, True).wait_recv()
-            self.core(3 + h, False).start()
+        me = self.me
+        self.got(self.DG, self.fd(0))
+        ref = self.view(me.z, 1 - me.y, me.x, me.c, 0)
+        ref[...] = ref[...] + self.fd(0)[...]
+        self.send(self.H + 2, ref, self.fxy(1, 0), self.py)
+        self.got(self.DG + 1, self.fd(1))
+        ref = self.view(me.z, me.y, 1 - me.x, me.c, 1)
+        ref[...] = ref[...] + self.fd(1)[...]
+        self.send(self.H + 3, ref, self.fxy(0, 1), self.px)
 
     def finish(self):
-        self.core(0, True).wait_recv()
-        for h in self.halves:
-            self.core(1 + h, True).wait_recv()
-            self.core(3 + h, True).wait_recv()
-
-    def drain(self):
-        for dz in range(1, self.me.nz):
-            self.along_z(dz, False).wait_send()
-        self.core(0, False).wait_send()
-        for h in self.halves:
-            self.second(h, False).wait_send()
-            self.third(h, False).wait_send()
-            self.core(1 + h, False).wait_send()
-            self.core(3 + h, False).wait_send()
+        me = self.me
+        self.got(self.H, self.fxy(0, 0))
+        self.got(self.H + 1, self.fxy(1, 1))
+        self.got(self.H + 2, self.fxy(1, 0))
+        self.got(self.H + 3, self.fxy(0, 1))
+        total = self.view(me.z, me.y, me.x, me.c, None)[...].astype(F32)
+        return total + self.fxy(0, None)[...].astype(F32) + self.fxy(1, None)[...].astype(F32)
 
 
 class Reduce:
@@ -245,7 +331,7 @@
         yv_h, yc_h, gv_h, gc_h, poolv_o, poolc_o, gwr_o, gws_o, gwe_o, small_o,
         wr, ws, we, par, mask, raw_v, raw_c, cpv, cpc, x, xt, cot, a1, a2, a3, gpre, ysv, ysc, gact,
         hv, hc, dv, dc, h2, h2t, ga1, gwr, gws, gwe,
-        fc_we, fc_ws, fc_wr, f3_we, f3_ws, f3_wr, f2_we, f2_ws, f2_wr, fz_we, fz_ws, fz_wr,
+        fc_we, fc_ws, fc_wr, f3_we, f3_ws, f3_wr, f2_we, f2_ws, f2_wr, fz_we, fz_ws, fz_wr, fp_we, fd_we, fh_we,
         p1, p3, mi1, mi2, mi3, cnt, ex1, ex2, ex3, bx1, bx2, bx3, tot1, tot2, tot3,
         pf, pb, pr, sb, rb,
         in_sem, out_sem, ag_s, ag_r, rs_s, rs_r, ex_s, ex_r, halo_s, halo_r, pool_s, pool_r, sm_s, sm_r,
@@ -260,6 +346,12 @@
     CH = 32
     chunks = [(s, 0 if s < pix_v else 1) for s in range(0, pix, CH)]
 
+    barrier = pltpu.get_barrier_semaphore()
+    peers = [{"dp": me.dp, "rows": (me.r + d) % n_rows} for d in range(1, n_rows)]
+    peers += [{"dp": (me.dp + d) % n_dp, "rows": me.r} for d in range(1, n_dp)]
+    for peer in peers:
+        pl.semaphore_signal(barrier, inc=1, device_id=peer, device_id_type=MESH)
+
     def fetch(k, views, crops):
         return [
             pltpu.make_async_copy(views.at[:, col], raw_v.at[col], in_sem.at[k, col]) for col in range(cols_v)
@@ -320,23 +412,20 @@
     cnt_own[1:2] = jnp.sum(mask[pix_v:pix], axis=0, keepdims=True)
     cnt_own[2:8] = jnp.zeros((6, 128), F32)
 
-    barrier = pltpu.get_barrier_semaphore()
-    peers = [{"dp": me.dp, "rows": (me.r + d) % n_rows} for d in range(1, n_rows)]
-    peers += [{"dp": (me.dp + d) % n_dp, "rows": me.r} for d in range(1, n_dp)]
-    for peer in peers:
-        pl.semaphore_signal(barrier, inc=1, device_id=peer, device_id_type=MESH)
     pl.semaphore_wait(barrier, len(peers))
 
-    def piece(k, view, halves=(0, 1)):
-        return Gather(me, view, ag_s.at[k], ag_r.at[k], halves)
-
+    def piece(k, view, halves=(0, 1), form=Gather):
+        return form(me, view, ag_s.at[k], ag_r.at[k], *(() if form is GatherPlane else (halves,)))
+
+    part = wide // 2
     small_piece = piece(0, lambda z, y, x, c, h: par.at[z, y, x, c], (0,))
     pieces = [piece(1, lambda z, y, x, c, h: wr.at[z, y, x, c, :, half(h, mid)])]
     for i in range(3):
         pieces.append(
             piece(2 + i, lambda z, y, x, c, h, i=i: ws.at[3 * i : 3 * i + 3, z, y, x, c, :, half(h, mid)])
         )
-    pieces.append(piece(5, lambda z, y, x, c, h: we.at[z, y, x, c, :, half(h, wide)]))
+    pieces.append(piece(5, lambda z, y, x, c, h: we.at[z, y, x, c, :, half(h, part, 0, part)]))
+    plane = piece(6, lambda z, y, x, c, h: we.at[z, y, x, c, :, half(h, part, part, part)], form=GatherPlane)
 
     def exchange(k, buf):
         def cp(d, recv):
@@ -358,7 +447,13 @@
 
         return send, wait, drain
 
-    exchanges = [exchange(k, b) for k, b in enumerate((cnt, ex1, ex2, ex3, bx1, bx2, bx3))]
+    exchanges = [
+        exchange(k, b)
+        for k, b in enumerate(
+            (cnt, ex1, ex2, ex3.at[0], ex3.at[1], bx1, bx2, bx3.at[0], bx3.at[1])
+        )
+    ]
+    CNT, EX1, EX2, EX3, BX1, BX2, BX3 = 0, 1, 2, 3, 5, 6, 7
 
     def rim(k, v, c):
         def cps(up):
@@ -441,21 +536,24 @@
         else:
             buf[me.r, pl.ds(4 * (j // tiles) + k, 1), lanes(j % tiles)] = value
 
-    def local_stats(a, buf, n_tiles):
+    def masked(s):
+        return jnp.concatenate([mask[s : s + CH]] * (TILE // 128), axis=1)
+
+    def local_stats(a, buf, n_tiles, first=0):
         def body(j, carry):
-            cols = lanes(j)
+            cols = lanes(j + first)
             for grp in (0, 1):
                 acc = jnp.zeros((8, TILE), F32)
                 for s, g in chunks:
                     if g == grp:
-                        acc = acc + fold(a[s : s + CH, cols] * mask[s : s + CH, 0:1])
+                        acc = acc + fold(a[s : s + CH, cols] * masked(s))
                 total = jnp.sum(acc, axis=0, keepdims=True)
                 n_own = jnp.maximum(cnt[me.r, grp : grp + 1, 0:1], 1.0)
                 mean = total / n_own
                 acc = jnp.zeros((8, TILE), F32)
                 for s, g in chunks:
                     if g == grp:
-                        d = (a[s : s + CH, cols] - mean) * mask[s : s + CH, 0:1]
+                        d = (a[s : s + CH, cols] - mean) * masked(s)
                         acc = acc + fold(d * d)
                 put(buf, j, 2 * grp, total)
                 put(buf, j, 2 * grp + 1, jnp.sum(acc, axis=0, keepdims=True))
@@ -466,7 +564,7 @@
         if n_tiles > 2:
             lax.fori_loop(0, n_tiles, body, 0)
 
-    def merge_stats(buf, mi):
+    def merge_stats(buf, mi, at=0):
         width = buf.shape[2]
         for hf in (0, 1):
             for grp in (0, 1):
@@ -478,18 +576,18 @@
                     n_i = cnt[i, grp : grp + 1, 0:1]
                     off = buf[i, k : k + 1] / jnp.maximum(n_i, 1.0) - mean
                     spread = spread + buf[i, k + 1 : k + 2] + n_i * (off * off)
-                mi[2 * grp : 2 * grp + 1, hf * width : (hf + 1) * width] = mean
-                mi[2 * grp + 1 : 2 * grp + 2, hf * width : (hf + 1) * width] = lax.rsqrt(
+                mi[2 * grp : 2 * grp + 1, at + hf * width : at + (hf + 1) * width] = mean
+                mi[2 * grp + 1 : 2 * grp + 2, at + hf * width : at + (hf + 1) * width] = lax.rsqrt(
                     spread / count[grp] + eps
                 )
 
-    def merge_grads(buf, tot):
+    def merge_grads(buf, tot, at=0):
         width = buf.shape[2]
         for hf in (0, 1):
             block = buf[0, 4 * hf : 4 * hf + 4]
             for i in range(1, n_rows):
                 block = block + buf[i, 4 * hf : 4 * hf + 4]
-            tot[0:4, hf * width : (hf + 1) * width] = block
+            tot[0:4, at + hf * width : at + (hf + 1) * width] = block
 
     def expand_params():
         blocks = par[...].reshape(n_dp * n_rows * 8, 128).astype(BF)
@@ -511,45 +609,49 @@
     def gain(out, i, cols):
         return out[i : i + 1, cols]
 
-    small_piece.start()
-    pieces[0].start()
-    exchanges[0][0]()
+    small_piece.start_z()
+    small_piece.start_xy()
+    pieces[0].start_z()
+    pieces[0].start_xy()
+    exchanges[CNT][0]()
+    plane.start()
+    for p in pieces[1:]:
+        p.start_xy()
     clear_rims(hv, hc)
     clear_rims(dv, dc)
     for cp in x_copies:
         cp.wait()
-
-    def step0(t):
-        pieces[t].got_z()
-        if t + 1 < len(pieces):
-            pieces[t + 1].start()
-        pieces[t].stage2()
-
     arrange(x)
     for cp in cot_copies:
         cp.start()
-    small_piece.got_z()
-    small_piece.stage2()
+
+    def step0(t):
+        pieces[t].got_z(1)
+        if t + 1 < len(pieces):
+            pieces[t + 1].start_z()
+        for k in range(2, me.nz):
+            pieces[t].got_z(k)
+
+    for k in range(1, me.nz):
+        small_piece.got_z(k)
     step0(0)
+    plane.diagonal()
+    small_piece.diagonal()
     for t in range(wide // TILE):
         xt[t * TILE : (t + 1) * TILE, :] = x[:, t * TILE : (t + 1) * TILE].T
-    small_piece.stage3()
     step0(1)
-    pieces[0].stage3()
-    small_piece.stage4()
+    pieces[0].diagonal()
+    small_piece.last()
     for cp in cot_copies:
         cp.wait()
     arrange(cot)
     step0(2)
-    pieces[1].stage3()
-    pieces[0].stage4()
+    pieces[1].diagonal()
+    pieces[0].last()
     small_piece.finish()
     expand_params()
-    step0(3)
-    pieces[2].stage3()
-    pieces[1].stage4()
     pieces[0].finish()
-    exchanges[0][1]()
+    exchanges[CNT][1]()
 
     def conv1(j, carry):
         w = wr[:, :, :, :, :, lanes(j)].reshape(wide, TILE)
@@ -558,12 +660,11 @@
 
     lax.fori_loop(0, mid // TILE, conv1, 0)
     local_stats(a1, ex1, mid // TILE)
-    exchanges[1][0]()
-    step0(4)
-    pieces[3].stage3()
-    pieces[2].stage4()
-    pieces[1].finish()
-    exchanges[1][1]()
+    exchanges[EX1][0]()
+    step0(3)
+    pieces[2].diagonal()
+    pieces[1].last()
+    exchanges[EX1][1]()
     merge_stats(ex1, mi1)
 
     def store_rows(v, c, s, cols, value):
@@ -582,7 +683,7 @@
             shift = gain(p1, i + 1, cols)
             for s, g in chunks:
                 zed = (a[s : s + CH, cols] - mean[g]) * scale[g] + shift
-                store(s, cols, (zed * sigmoid(zed) * mask[s : s + CH, 0:1]).astype(BF))
+                store(s, cols, (zed * sigmoid(zed) * masked(s)).astype(BF))
             return carry
 
         for j in range(mid // TILE):
@@ -590,37 +691,41 @@
 
     act(a1, mi1, 0, lambda s, cols, value: store_rows(hv, hc, s, cols, value))
     rim_h[0]()
-    pieces[4].stage3()
-    pieces[3].stage4()
+    step0(4)
+    plane.plane()
+    pieces[3].diagonal()
+    pieces[2].last()
+    pieces[1].finish()
+    rim_h[1]()
+
+    def windows(v, c, dy, dx):
+        left = [v[r + dy, dx * maps_v : dx * maps_v + row_v, :] for r in (0, 1)]
+        return jnp.concatenate(left + [c[dy, dx * maps_c : dx * maps_c + row_c, :]], axis=0)
+
+    def conv2(dy):
+        left = jnp.concatenate([windows(hv, hc, dy, dx) for dx in range(3)], axis=1)
+        for j in range(mid // TILE):
+            w = ws[3 * dy : 3 * dy + 3, :, :, :, :, :, lanes(j)].reshape(3 * mid, TILE)
+            part_sum = dot(left, w)
+            a2[:, lanes(j)] = part_sum if dy == 0 else a2[:, lanes(j)] + part_sum
+
+    conv2(0)
+    pieces[4].diagonal()
     pieces[2].finish()
-    pieces[4].stage4()
+    conv2(1)
+    pieces[3].last()
     pieces[3].finish()
-    rim_h[1]()
-
-    def conv2(tap, carry):
-        dy, dx = tap // 3, tap % 3
-        w = ws[tap].reshape(mid, mid)
-        for r in (0, 1):
-            left = hv[r + dy, pl.ds(pl.multiple_of(dx * maps_v, maps_v), row_v), :]
-            block = a2.at[r * row_v : (r + 1) * row_v]
-            block[...] = block[...] + dot(left, w)
-        left = hc[dy, pl.ds(pl.multiple_of(dx * maps_c, maps_c), row_c), :]
-        block = a2.at[pix_v:pix]
-        block[...] = block[...] + dot(left, w)
-        return carry
-
-    a2[...] = jnp.zeros(a2.shape, F32)
-    lax.fori_loop(0, 9, conv2, 0)
+    conv2(2)
     local_stats(a2, ex2, mid // TILE)
-    exchanges[2][0]()
-    exchanges[2][1]()
+    exchanges[EX2][0]()
+    pieces[4].last()
+    exchanges[EX2][1]()
     merge_stats(ex2, mi2)
 
     def store_h2(s, cols, value):
         h2[s : s + CH, cols] = value
 
     act(a2, mi2, 2, store_h2)
-    pieces[4].finish()
     for cp in pool_copies:
         cp.wait()
 
@@ -629,12 +734,19 @@
         a3[:, lanes(j)] = dot(h2[...], w)
         return carry
 
-    lax.fori_loop(0, wide // TILE, conv3, 0)
-    local_stats(a3, ex3, wide // TILE)
-    exchanges[3][0]()
+    tiles = wide // TILE // 2
+    pieces[4].finish()
+    lax.fori_loop(0, tiles, conv3, 0)
+    local_stats(a3, ex3.at[0], tiles)
+    exchanges[EX3][0]()
+    plane.last()
+    plane.finish()
+    lax.fori_loop(tiles, 2 * tiles, conv3, 0)
+    local_stats(a3, ex3.at[1], tiles, tiles)
+    exchanges[EX3 + 1][0]()
     h2t[...] = h2[...].T
-    exchanges[3][1]()
-    merge_stats(ex3, mi3)
+    exchanges[EX3][1]()
+    merge_stats(ex3.at[0], mi3)
 
     def out_copies(j, slot, views, crops):
         return [
@@ -650,19 +762,24 @@
             for k in (0, 1):
                 ysc[slot, at : at + CH, col, k, :] = value[:, k * 128 : (k + 1) * 128]
 
-    def last(jj, carry):
+    def last(q, jj, carry):
         for slot in (0, 1):
             j = 2 * jj + slot
             cols = lanes(j)
 
-            @pl.when(jj > 0)
-            def _():
+            def free_slot():
                 for cp in out_copies(j, slot, yv_h, yc_h):
                     cp.wait()
 
+            if q > 0:
+                free_slot()
+            else:
+                pl.when(jj > 0)(free_slot)
+
             mean = [mi3[2 * g : 2 * g + 1, cols] for g in (0, 1)]
             inv = [mi3[2 * g + 1 : 2 * g + 2, cols] for g in (0, 1)]
-            gn, sh = gain(p3, 4, cols), gain(p3, 5, cols)
+            scale = [inv[g] * gain(p3, 4, cols) for g in (0, 1)]
+            sh = gain(p3, 5, cols)
             sums = [jnp.zeros((8, TILE), F32) for _ in range(4)]
             pooled = [jnp.zeros((CH, TILE), F32) for _ in range((maps_v + maps_c) // CH)]
             per_v, per_c = CH // cpv.shape[1], CH // cpc.shape[1]
@@ -676,19 +793,22 @@
             for s, g in chunks:
                 which = (s % maps_v) // CH if g == 0 else (maps_v + (s - pix_v) % maps_c) // CH
                 rows = slice(s, s + CH)
-                m = mask[rows, 0:1]
-                nh = (a3[rows, cols] - mean[g]) * inv[g]
-                pre = x[rows, cols].astype(F32) + (nh * gn + sh)
+                m = masked(s)
+                off = a3[rows, cols] - mean[g]
+                pre = x[rows, cols].astype(F32) + (off * scale[g] + sh)
                 sig = sigmoid(pre)
-                out = pre * sig * m
+                act_out = pre * sig
+                out = act_out * m
                 store_out(slot, s, out)
                 pooled[which] = pooled[which] + out
-                gp = (cot[rows, cols].astype(F32) + cps[which]) * m * (sig * (1.0 + pre * (1.0 - sig)))
+                slope = act_out + sig * (1.0 - act_out)
+                gp = (cot[rows, cols].astype(F32) + cps[which]) * m * slope
                 gpre[rows, cols] = gp
-                sums[2 * g] = sums[2 * g] + fold(gp * nh)
+                sums[2 * g] = sums[2 * g] + fold(gp * off)
                 sums[2 * g + 1] = sums[2 * g + 1] + fold(gp)
             for k in range(4):
-                put(bx3, j, k, jnp.sum(sums[k], axis=0, keepdims=True))
+                total = jnp.sum(sums[k], axis=0, keepdims=True)
+                put(bx3.at[q], j - q * tiles, k, total * inv[k // 2] if k % 2 == 0 else total)
             for i, value in enumerate(pooled):
                 pf[i * CH : (i + 1) * CH, cols] = value
                 pb[i * CH : (i + 1) * CH, cols] = value.astype(BF)
@@ -696,53 +816,64 @@
                 cp.start()
         return carry
 
-    lax.fori_loop(0, wide // TILE // 2, last, 0)
-    exchanges[6][0]()
-
     core_peer = {"dp": me.dp, "rows": me.x * 2 + 1 - me.c}
     chip_peer = {"dp": me.dp, "rows": (1 - me.x) * 2 + me.c}
     pool_core = remote(pb, pr.at[0], pool_s.at[0], pool_r.at[0], core_peer)
+    lax.fori_loop(0, tiles // 2, functools.partial(last, 0), 0)
+    exchanges[BX3][0]()
+    exchanges[EX3 + 1][1]()
+    merge_stats(ex3.at[1], mi3, wide // 2)
+    lax.fori_loop(tiles // 2, tiles, functools.partial(last, 1), 0)
+    exchanges[BX3 + 1][0]()
     pool_core.start()
-    exchanges[6][1]()
-    merge_grads(bx3, tot3)
 
     def coefs(mi, tot, gn, cols):
         out = []
         for g in (0, 1):
             mean, inv = mi[2 * g : 2 * g + 1, cols], mi[2 * g + 1 : 2 * g + 2, cols]
             dg, ds = tot[2 * g : 2 * g + 1, cols], tot[2 * g + 1 : 2 * g + 2, cols]
-            out.append((mean, inv, gn * inv, ds / count[g], dg / count[g]))
+            out.append((mean, gn * inv, ds / count[g], dg / count[g] * inv))
         return out
+
+    def norm_back(gz, a, co, s, cols):
+        mean, k0, k1, k2 = co
+        return (k0 * (gz - k1 - (a[s : s + CH, cols] - mean) * k2) * masked(s)).astype(BF)
 
     def grad_three(j, carry):
         cols = lanes(j)
         co = coefs(mi3, tot3, gain(p3, 4, cols), cols)
         for s, g in chunks:
-            rows = slice(s, s + CH)
-            mean, inv, k0, k1, k2 = co[g]
-            nh = (a3[rows, cols] - mean) * inv
-            cot[rows, cols] = (k0 * (gpre[rows, cols] - k1 - nh * k2) * mask[rows, 0:1]).astype(BF)
+            cot[s : s + CH, cols] = norm_back(gpre[s : s + CH, cols], a3, co[g], s, cols)
         gwe[:, :, :, :, :, cols] = (
             dot(h2t[...], cot[:, cols]).astype(BF).reshape(gwe.shape[:5] + (TILE,))
         )
         return carry
 
-    lax.fori_loop(0, wide // TILE, grad_three, 0)
+    q_first = ReducePlane(
+        me,
+        lambda z, y, x, c, h: gwe.at[z, y, x, c, :, half(h, part, 0, part)],
+        lambda: fc_we.at[:, :, :, :, 0:part],
+        lambda k: fp_we.at[k],
+        lambda h: fd_we.at[h],
+        lambda k, h: fh_we.at[k, :, half(h, part)],
+        rs_s.at[0],
+        rs_r.at[0],
+    )
 
     def reducer(k, view, fc, f3, f2, fz):
         return Reduce(me, view, fc, f3, f2, fz, rs_s.at[k], rs_r.at[k])
 
     q_we = reducer(
-        0,
-        lambda z, y, x, c, h: gwe.at[z, y, x, c, :, half(h, wide)],
-        lambda z, y, x, h: fc_we.at[z, y, x, :, half(h, wide)],
+        1,
+        lambda z, y, x, c, h: gwe.at[z, y, x, c, :, half(h, part, part, part)],
+        lambda z, y, x, h: fc_we.at[z, y, x, :, half(h, part, part, part)],
         lambda h: f3_we.at[h],
         lambda h: f2_we.at[h],
         lambda k: fz_we.at[k],
     )
     q_ws = [
         reducer(
-            1 + i,
+            2 + i,
             lambda z, y, x, c, h, i=i: gws.at[3 * i : 3 * i + 3, z, y, x, c, :, half(h, mid)],
             lambda z, y, x, h, i=i: fc_ws.at[3 * i : 3 * i + 3, z, y, x, :, half(h, mid)],
             lambda h, i=i: f3_ws.at[h, 3 * i : 3 * i + 3],
@@ -751,15 +882,28 @@
         )
         for i in range(3)
     ]
-    q_wr = reducer(
-        4,
-        lambda z, y, x, c, h: gwr.at[z, y, x, c, :, half(h, mid)],
-        lambda z, y, x, h: fc_wr.at[z, y, x, :, half(h, mid)],
-        lambda h: f3_wr.at[h],
-        lambda h: f2_wr.at[h],
-        lambda k: fz_wr.at[k],
-    )
+    few = wr.shape[4] // 2
+    q_wr = [
+        reducer(
+            5 + i,
+            lambda z, y, x, c, h, i=i: gwr.at[z, y, x, c, i * few : (i + 1) * few, half(h, mid)],
+            lambda z, y, x, h, i=i: fc_wr.at[z, y, x, i * few : (i + 1) * few, half(h, mid)],
+            lambda h, i=i: f3_wr.at[h, :, :, i * few : (i + 1) * few],
+            lambda h, i=i: f2_wr.at[h, :, i * few : (i + 1) * few],
+            lambda k, i=i: fz_wr.at[k, i * few : (i + 1) * few],
+        )
+        for i in range(2)
+    ]
+
+    exchanges[BX3][1]()
+    merge_grads(bx3.at[0], tot3)
+    lax.fori_loop(0, tiles, grad_three, 0)
+    q_first.start()
+    exchanges[BX3 + 1][1]()
+    merge_grads(bx3.at[1], tot3, wide // 2)
+    lax.fori_loop(tiles, 2 * tiles, grad_three, 0)
     q_we.start()
+    q_first.stage2()
 
     def grad_act(gh, a, mi, i, buf, j):
         cols = lanes(j)
@@ -768,15 +912,17 @@
         for s, g in chunks:
             rows = slice(s, s + CH)
             mean, inv = mi[2 * g : 2 * g + 1, cols], mi[2 * g + 1 : 2 * g + 2, cols]
-            nh = (a[rows, cols] - mean) * inv
-            zed = nh * gn + sh
+            off = a[rows, cols] - mean
+            zed = off * (inv * gn) + sh
             sig = sigmoid(zed)
-            gz = gh[rows, cols] * mask[rows, 0:1] * (sig * (1.0 + zed * (1.0 - sig)))
+            gz = gh[rows, cols] * masked(s) * (sig * (1.0 + zed * (1.0 - sig)))
             gh[rows, cols] = gz
-            sums[2 * g] = sums[2 * g] + fold(gz * nh)
+            sums[2 * g] = sums[2 * g] + fold(gz * off)
             sums[2 * g + 1] = sums[2 * g + 1] + fold(gz)
         for k in range(4):
-            put(buf, j, k, jnp.sum(sums[k], axis=0, keepdims=True))
+            total = jnp.sum(sums[k], axis=0, keepdims=True)
+            inv = mi[2 * (k // 2) + 1 : 2 * (k // 2) + 2, cols]
+            put(buf, j, k, total * inv if k % 2 == 0 else total)
 
     for j in range(mid // TILE):
         w = tile_rows(we, j).reshape(TILE, wide)
@@ -795,14 +941,14 @@
     for j in range(mid // TILE):
         ghs.j = j
         grad_act(ghs, a2, mi2, 2, bx2, j)
-    exchanges[5][0]()
+    exchanges[BX2][0]()
     q_we.stage2()
     pool_core.wait()
     pf[...] = pf[...] + pr[0].astype(F32)
     pb[...] = pf[...].astype(BF)
     pool_chip = remote(pb, pr.at[1], pool_s.at[1], pool_r.at[1], chip_peer)
     pool_chip.start()
-    exchanges[5][1]()
+    exchanges[BX2][1]()
     merge_grads(bx2, tot2)
 
     def grad_norm_all(a, mi, tot, i, store):
@@ -811,67 +957,52 @@
             cols = lanes(j)
             co = coefs(mi, tot, gain(p1, i, cols), cols)
             for s, g in chunks:
-                rows = slice(s, s + CH)
-                mean, inv, k0, k1, k2 = co[g]
-                nh = (a[rows, cols] - mean) * inv
-                value = k0 * (ghs[rows, cols] - k1 - nh * k2) * mask[rows, 0:1]
-                store(s, cols, value.astype(BF))
+                store(s, cols, norm_back(ghs[s : s + CH, cols], a, co[g], s, cols))
 
     grad_norm_all(a2, mi2, tot2, 2, lambda s, cols, value: store_rows(dv, dc, s, cols, value))
     rim_d[0]()
 
     def grad_taps(dy):
-        def body(dx, carry):
-            tap = 3 * dy + dx
-            total = dot_r(
-                hc[dy, pl.ds(pl.multiple_of(dx * maps_c, maps_c), row_c), :],
-                dc[1, maps_c : maps_c + row_c],
-            )
-            for r in (0, 1):
-                total = total + dot_r(
-                    hv[r + dy, pl.ds(pl.multiple_of(dx * maps_v, maps_v), row_v), :],
-                    dv[1 + r, maps_v : maps_v + row_v],
-                )
-            gws[tap] = total.astype(BF).reshape(gws.shape[1:])
-            return carry
-
-        lax.fori_loop(0, 3, body, 0)
+        right = windows(dv, dc, 1, 1)
+        for dx in range(3):
+            total = dot_r(windows(hv, hc, dy, dx), right)
+            gws[3 * dy + dx] = total.astype(BF).reshape(gws.shape[1:])
 
     grad_taps(0)
     q_ws[0].start()
-    q_we.stage3()
+    q_first.stage3()
     grad_taps(1)
     q_ws[1].start()
     q_ws[0].stage2()
+    q_we.stage3()
     grad_taps(2)
     q_ws[2].start()
     q_ws[1].stage2()
+    q_first.stage4()
     rim_d[1]()
 
-    gact[...] = jnp.zeros(gact.shape, F32)
-
-    def conv2_back(tap, carry):
-        dy, dx = 2 - tap // 3, 2 - tap % 3
+    def conv2_back(dy):
+        left = jnp.concatenate([windows(dv, dc, 2 - dy, 2 - dx) for dx in range(3)], axis=1)
         for j in range(mid // TILE):
-            w = tile_rows(ws.at[tap], j).reshape(TILE, mid)
-            for r in (0, 1):
-                left = dv[r + dy, pl.ds(pl.multiple_of(dx * maps_v, maps_v), row_v), :]
-                block = gact.at[j, r * row_v : (r + 1) * row_v]
-                block[...] = block[...] + dot_t(left, w)
-            left = dc[dy, pl.ds(pl.multiple_of(dx * maps_c, maps_c), row_c), :]
-            block = gact.at[j, pix_v:pix]
-            block[...] = block[...] + dot_t(left, w)
-        return carry
-
-    lax.fori_loop(0, 9, conv2_back, 0)
+            w = jnp.concatenate(
+                [tile_rows(ws.at[3 * dy + dx], j).reshape(TILE, mid) for dx in range(3)], axis=1
+            )
+            part_sum = dot_t(left, w)
+            gact[j] = part_sum if dy == 0 else gact[j] + part_sum
+
+    conv2_back(0)
+    q_ws[0].stage3()
+    q_ws[2].stage2()
+    conv2_back(1)
+    q_we.stage4()
+    conv2_back(2)
     for j in range(mid // TILE):
         ghs.j = j
         grad_act(ghs, a1, mi1, 0, bx1, j)
-    exchanges[4][0]()
-    q_we.stage4()
-    q_ws[0].stage3()
-    q_ws[2].stage2()
-    exchanges[4][1]()
+    exchanges[BX1][0]()
+    q_ws[1].stage3()
+    gwe_o[:, 0:part] = q_first.finish()
+    exchanges[BX1][1]()
     merge_grads(bx1, tot1)
 
     def store_ga1(s, cols, value):
@@ -881,9 +1012,10 @@
     for t in range(wide // TILE):
         block = dot(xt[t * TILE : (t + 1) * TILE, :], ga1[...]).astype(BF)
         gwr[t // 2, t % 2] = block.reshape(gwr.shape[2:])
-    q_wr.start()
-    q_ws[1].stage3()
+    for q in q_wr:
+        q.start()
     q_ws[0].stage4()
+    q_ws[2].stage3()
 
     n_dev = n_dp * n_rows
 
@@ -935,21 +1067,27 @@
         for cp in out_copies(j, slot, gv_h, gc_h):
             cp.start()
 
-    steps = [
-        q_wr.stage2, q_ws[2].stage3, q_ws[1].stage4, q_wr.stage3, q_ws[2].stage4, q_wr.stage4,
-    ]
-    for j in range(wide // TILE):
+    q_wr[0].stage2()
+    q_wr[1].stage2()
+    grad_in(0)
+    grad_in(1)
+    q_ws[1].stage4()
+    grad_in(2)
+    q_wr[0].stage3()
+    q_wr[1].stage3()
+    grad_in(3)
+    q_ws[2].stage4()
+    grad_in(4)
+    q_wr[0].stage4()
+    q_wr[1].stage4()
+    for j in range(5, wide // TILE):
         grad_in(j)
-        if j < 3:
-            steps[j]()
-    gwe_o[...] = q_we.finish()
+    gwe_o[:, part:wide] = q_we.finish()
     gws_o[0:3] = q_ws[0].finish()
     pool_chip.wait()
     for out, at, maps, valid in ((poolv_o, 0, maps_v, valid_v), (poolc_o, maps_v, maps_c, valid_c)):
         total = pf[at : at + maps] + pr[1, at : at + maps].astype(F32)
         out[...] = (total * (1.0 / valid)).reshape(out.shape)
-    for step in steps[3:]:
-        step()
     total = sb[me.dp]
     for d in range(1, n_dp):
         small_cp(d, True).wait_recv()
@@ -957,22 +1095,51 @@
     small_o[...] = total
     gws_o[3:6] = q_ws[1].finish()
     gws_o[6:9] = q_ws[2].finish()
-    gwr_o[...] = q_wr.finish()
+    for i, q in enumerate(q_wr):
+        gwr_o[i * few : (i + 1) * few] = q.finish()
 
     for j in (wide // TILE - 2, wide // TILE - 1):
         for cp in out_copies(j, j % 2, gv_h, gc_h):
             cp.wait()
     small_piece.drain()
-    for p in pieces:
+    for p in pieces + [plane]:
         p.drain()
     for e in exchanges:
         e[2]()
     rim_h[2]()
     rim_d[2]()
-    for q in [q_we] + q_ws + [q_wr]:
+    for q in [q_first, q_we] + q_ws + q_wr:
         q.drain()
     for d in range(1, n_dp):
         small_cp(d, False).wait_send()
+
+
+def hand_over(*refs):
+    n = (len(refs) - 8) // 3
+    srcs, small, dsts = refs[:n], refs[n], refs[n + 1 : 2 * n + 1]
+    cuts, bufs, sem = refs[2 * n + 1 : 2 * n + 7], refs[2 * n + 7 : -1], refs[-1]
+    parts = 4
+    ways = []
+    for i, (src, buf, dst) in enumerate(zip(srcs, bufs, dsts)):
+        count = parts if src.shape[0] % parts == 0 else 1
+        per = src.shape[0] // count
+        for k in range(count):
+            rows = slice(k * per, (k + 1) * per)
+            ways.append(
+                (
+                    pltpu.make_async_copy(src.at[rows], buf.at[rows], sem.at[0, i, k]),
+                    pltpu.make_async_copy(buf.at[rows], dst.at[rows], sem.at[1, i, k]),
+                )
+            )
+    for inward, _ in ways:
+        inward.start()
+    for i, ref in enumerate(cuts):
+        ref[...] = small[i : i + 1, 0 : ref.shape[1]]
+    for inward, outward in ways:
+        inward.wait()
+        outward.start()
+    for _, outward in ways:
+        outward.wait()
 
 
 def block_step(n_dp, n_rows, xv, xc, mv, mc, wr, ws, we, g1, s1, g2, s2, g3, s3, cv, cc, cpv, cpc):
@@ -1011,19 +1178,20 @@
         V((pix, mid), BF), V((mid, pix), BF), V((pix, mid), BF),
         V(grid4 + (s_wr, mid), BF), V((9,) + grid4 + (s_we, mid), BF), V(grid4 + (s_we, wide), BF),
         V((nz, 2, nx, s_we, wide), BF), V((9, nz, 2, nx, s_we, mid), BF), V((nz, 2, nx, s_wr, mid), BF),
-        V((2, nz, 2, s_we, wide // 2), BF), V((2, 9, nz, 2, s_we, mid // 2), BF), V((2, nz, 2, s_wr, mid // 2), BF),
-        V((2, nz, s_we, wide // 2), BF), V((2, 9, nz, s_we, mid // 2), BF), V((2, nz, s_wr, mid // 2), BF),
-        V((nz - 1, s_we, wide), BF), V((nz - 1, 9, s_we, mid), BF), V((nz - 1, s_wr, mid), BF),
+        V((2, nz, 2, s_we, wide // 4), BF), V((2, 9, nz, 2, s_we, mid // 2), BF), V((2, nz, 2, s_wr, mid // 2), BF),
+        V((2, nz, s_we, wide // 4), BF), V((2, 9, nz, s_we, mid // 2), BF), V((2, nz, s_wr, mid // 2), BF),
+        V((nz - 1, s_we, wide // 2), BF), V((nz - 1, 9, s_we, mid), BF), V((nz - 1, s_wr, mid), BF),
+        V((nz - 1, 2, nx, s_we, wide // 2), BF), V((2, s_we, wide // 4), BF), V((2, s_we, wide // 2), BF),
         V((8, mid), F32), V((8, wide), F32),
         V((4, mid), F32), V((4, mid), F32), V((4, wide), F32),
         V((n_rows, 8, 128), F32),
-        V((n_rows, 8, mid // 2), F32), V((n_rows, 8, mid // 2), F32), V((n_rows, 8, wide // 2), F32),
-        V((n_rows, 8, mid // 2), F32), V((n_rows, 8, mid // 2), F32), V((n_rows, 8, wide // 2), F32),
+        V((n_rows, 8, mid // 2), F32), V((n_rows, 8, mid // 2), F32), V((2, n_rows, 8, wide // 4), F32),
+        V((n_rows, 8, mid // 2), F32), V((n_rows, 8, mid // 2), F32), V((2, n_rows, 8, wide // 4), F32),
         V((4, mid), F32), V((4, mid), F32), V((4, wide), F32),
         V((maps_v + maps_c, wide), F32), V((maps_v + maps_c, wide), BF), V((2, maps_v + maps_c, wide), BF),
         V((n_dp, 8, 128), F32), V((n_dp - 1, 8, 128), F32),
-        D((3, cols_v + 1)), D((2, 2)), D((6, 12)), D((6, 12)), D((5, 5 + nz)), D((5, 5 + nz)),
-        D((7, n_rows - 1)), D((7, n_rows - 1)), D((2, 4)), D((2, 4)), D((2,)), D((2,)), D((n_dp - 1,)), D((n_dp - 1,)),
+        D((3, cols_v + 1)), D((2, 2)), D((7, 5 * nz + 4)), D((7, 5 * nz + 4)), D((7, 6 + nz)), D((7, 6 + nz)),
+        D((9, n_rows - 1)), D((9, n_rows - 1)), D((2, 4)), D((2, 4)), D((2,)), D((2,)), D((n_dp - 1,)), D((n_dp - 1,)),
     ]
     out_v = jax.ShapeDtypeStruct((maps_v, cols_v, 2, wide), F32)
     out_c = jax.ShapeDtypeStruct((maps_c, cols_c, wide // TILE, TILE // 128, 128), F32)
@@ -1047,7 +1215,19 @@
         g1.reshape(1, -1), s1.reshape(1, -1), g2.reshape(1, -1), s2.reshape(1, -1),
         g3.reshape(1, -1), s3.reshape(1, -1),
     )
-    yv, yc, gv, gc, pool_v, pool_c, gwr, gws, gwe, small = outs
+    e = mid // (n_dp * n_rows)
+    f = wide // (n_dp * n_rows)
+    big, shapes = outs[:-1], [jax.ShapeDtypeStruct(o.shape, F32) for o in outs[:-1]]
+    res = pl.pallas_call(
+        hand_over,
+        out_shape=shapes + [jax.ShapeDtypeStruct((1, w), F32) for w in (e, e, e, e, f, f)],
+        in_specs=[hbm] * len(big) + [vm],
+        out_specs=[hbm] * len(big) + [vm] * 6,
+        scratch_shapes=[V(o.shape, F32) for o in big] + [D((2, len(big), 4))],
+        compiler_params=pltpu.CompilerParams(vmem_limit_bytes=62 << 20),
+    )(*outs)
+    yv, yc, gv, gc, pool_v, pool_c, gwr, gws, gwe = res[:9]
+    small = [r.reshape(-1) for r in res[9:]]
 
     def views_out(t):
         return t.reshape(img, views, cols_v, rows_v, wide).transpose(0, 1, 3, 2, 4)
@@ -1055,14 +1235,12 @@
     def crops_out(t):
         return t.reshape(img, crops, 1, cols_c, wide)
 
-    e = mid // (n_dp * n_rows)
-    f = wide // (n_dp * n_rows)
     return (
         views_out(yv), crops_out(yc),
         pool_v, pool_c,
         views_out(gv), crops_out(gc),
         gwr, gws.reshape(3, 3, s_we, mid), gwe,
-        small[0, :e], small[1, :e], small[2, :e], small[3, :e], small[4, :f], small[5, :f],
+        *small,
     )
 
 

time: 174 us -> 151 us (0.87)
  local copies, waits for them, and re-layouts: 17.7 us -> 0 us
  Pallas kernels: 156 us -> 150 us
    pallas_call x1, Pallas kernels: 156 us -> 139 us  [block_step(): pl.pallas_call(functools.partial(kernel, n_dp, n_rows, (maps_v, cols_v, m...]
    unnamed x25 -> x0, local copies, waits for them, and re-layouts: 15 us -> none
    pallas_call x0 -> x1, Pallas kernels: none -> 10.5 us  [block_step(): pl.pallas_call(hand_over, out_shape=shapes + [jax.ShapeDtypeStruct((1, w)...]
    squeeze x2 -> x0, local copies, waits for them, and re-layouts: 2.62 us -> none  [the longest x1 1.35 us: block_step(): small[3, :e]]
where the time goes in v1:
time: 151 us; the launch traced here: 150 us
  Pallas kernels  150 us (99%)
    pallas_call x1, Pallas kernels, block_step(): pl.pallas_call(functools.partial(kernel, n_dp, n_rows, (maps_v, cols_v, m...  139 us
    pallas_call x1, Pallas kernels, block_step(): pl.pallas_call(hand_over, out_shape=shapes + [jax.ShapeDtypeStruct((1, w)...  10.5 us

profile of v1, /device:TPU:0, one launch (start us, length us, event | category | flops | bytes accessed | tf_op | source)
XLA Modules:
  0.0 150.4 jit_solution(18324994624710489506)
XLA Ops:
  0.7 139.1 %shard_map.280 = (f32[32,7,2,2048]{3,2,1,0:T(2,128)}, f32[64,3,8,2,128]{4,3,2,1,0:T(2,128)}, f32[32,7,2,2048]{3,2,1,0:T(2,128)}, f32[64,3,8,2,128]{4,3,2,1,0:T(2...) custom-call(bf16[32,7,2,2048]{3,2,1,0:T(2,128)(2,1)} %bitcast.40, ...), custom_call_target="tpu_custom_call" | custom-call | tf_op jit(solution)/shard_map/pallas_call | solution.py:1198
  139.8 10.5 %shard_map.281 = (f32[32,7,2,2048]{3,2,1,0:T(2,128)}, f32[64,3,8,2,128]{4,3,2,1,0:T(2,128)}, f32[32,7,2,2048]{3,2,1,0:T(2,128)}, f32[64,3,8,2,128]{4,3,2,1,0:T(2...) custom-call(f32[32,7,2,2048]{3,2,1,0:T(2,128)} %get-tuple-element.40, ...), custom_call_target="tpu_custom_call" | custom-call | tf_op jit(solution)/shard_map/pallas_call | solution.py:1221

commit v2 on v1

--- a/solution.py
+++ b/solution.py
@@ -41,6 +41,10 @@
 
 def sigmoid(v):
     return 0.5 * jnp.tanh(0.5 * v) + 0.5
+
+
+def uneven(h, width):
+    return ALL if h is None else slice(h * (width // 4), width if h else width // 4)
 
 
 class Place:
@@ -326,10 +330,10 @@
 
 def kernel(n_dp, n_rows, sizes, *refs):
     (
-        xv_h, xc_h, cv_h, cc_h, cpv_h, cpc_h, mv_in, mc_in, wr_in, ws_in, we_in,
+        xv_h, xc_h, cv_h, cc_h, cpv_h, cpc_h, wr_h, ws_h, we_h, mv_in, mc_in,
         g1_in, s1_in, g2_in, s2_in, g3_in, s3_in,
         yv_h, yc_h, gv_h, gc_h, poolv_o, poolc_o, gwr_o, gws_o, gwe_o, small_o,
-        wr, ws, we, par, mask, raw_v, raw_c, cpv, cpc, x, xt, cot, a1, a2, a3, gpre, ysv, ysc, gact,
+        wr_in, ws_in, we_in, wr, ws, we, par, mask, raw_v, raw_c, cpv, cpc, x, xt, cot, a1, a2, a3, gpre, ysv, ysc, gact,
         hv, hc, dv, dc, h2, h2t, ga1, gwr, gws, gwe,
         fc_we, fc_ws, fc_wr, f3_we, f3_ws, f3_wr, f2_we, f2_ws, f2_wr, fz_we, fz_ws, fz_wr, fp_we, fd_we, fh_we,
         p1, p3, mi1, mi2, mi3, cnt, ex1, ex2, ex3, bx1, bx2, bx3, tot1, tot2, tot3,
@@ -376,13 +380,14 @@
         pltpu.make_async_copy(cpv_h, cpv, in_sem.at[2, 0]),
         pltpu.make_async_copy(cpc_h, cpc, in_sem.at[2, 1]),
     ]
-    for cp in x_copies + pool_copies:
+    weight_copies = [
+        pltpu.make_async_copy(src, dst, in_sem.at[2, 2 + i])
+        for i, (src, dst) in enumerate(((wr_h, wr_in), (ws_h, ws_in), (we_h, we_in)))
+    ]
+    for cp in weight_copies + x_copies + pool_copies:
         cp.start()
 
     here = (me.z, me.y, me.x, me.c)
-    wr[here] = wr_in[...].astype(BF)
-    ws[(ALL,) + here] = ws_in[...].astype(BF)
-    we[here] = we_in[...].astype(BF)
     own = par.at[here]
     own[...] = jnp.zeros(own.shape, F32)
     for i, ref in enumerate((g1_in, s1_in, g2_in, s2_in, g3_in, s3_in)):
@@ -412,6 +417,12 @@
     cnt_own[1:2] = jnp.sum(mask[pix_v:pix], axis=0, keepdims=True)
     cnt_own[2:8] = jnp.zeros((6, 128), F32)
 
+    for cp in weight_copies:
+        cp.wait()
+    wr[here] = wr_in[...].astype(BF)
+    ws[(ALL,) + here] = ws_in[...].astype(BF)
+    we[here] = we_in[...].astype(BF)
+
     pl.semaphore_wait(barrier, len(peers))
 
     def piece(k, view, halves=(0, 1), form=Gather):
@@ -422,7 +433,7 @@
     pieces = [piece(1, lambda z, y, x, c, h: wr.at[z, y, x, c, :, half(h, mid)])]
     for i in range(3):
         pieces.append(
-            piece(2 + i, lambda z, y, x, c, h, i=i: ws.at[3 * i : 3 * i + 3, z, y, x, c, :, half(h, mid)])
+            piece(2 + i, lambda z, y, x, c, h, i=i: ws.at[3 * i : 3 * i + 3, z, y, x, c, :, uneven(h, mid)])
         )
     pieces.append(piece(5, lambda z, y, x, c, h: we.at[z, y, x, c, :, half(h, part, 0, part)]))
     plane = piece(6, lambda z, y, x, c, h: we.at[z, y, x, c, :, half(h, part, part, part)], form=GatherPlane)
@@ -658,7 +669,8 @@
         a1[:, lanes(j)] = dot(x[...], w)
         return carry
 
-    lax.fori_loop(0, mid // TILE, conv1, 0)
+    for j in range(mid // TILE):
+        conv1(j, 0)
     local_stats(a1, ex1, mid // TILE)
     exchanges[EX1][0]()
     step0(3)
@@ -736,12 +748,14 @@
 
     tiles = wide // TILE // 2
     pieces[4].finish()
-    lax.fori_loop(0, tiles, conv3, 0)
+    for j in range(tiles):
+        conv3(j, 0)
     local_stats(a3, ex3.at[0], tiles)
     exchanges[EX3][0]()
     plane.last()
     plane.finish()
-    lax.fori_loop(tiles, 2 * tiles, conv3, 0)
+    for j in range(tiles, 2 * tiles):
+        conv3(j, 0)
     local_stats(a3, ex3.at[1], tiles, tiles)
     exchanges[EX3 + 1][0]()
     h2t[...] = h2[...].T
@@ -818,7 +832,11 @@
 
     core_peer = {"dp": me.dp, "rows": me.x * 2 + 1 - me.c}
     chip_peer = {"dp": me.dp, "rows": (1 - me.x) * 2 + me.c}
-    pool_core = remote(pb, pr.at[0], pool_s.at[0], pool_r.at[0], core_peer)
+    share = pb.shape[0] // 2
+    mine, others = pl.ds(me.c * share, share), pl.ds((1 - me.c) * share, share)
+    pool_core = remote(pb.at[others], pr.at[0], pool_s.at[0], pool_r.at[0], core_peer)
+    pool_chip = remote(pb.at[mine], pr.at[1], pool_s.at[1], pool_r.at[1], chip_peer)
+    pool_back = remote(pb.at[mine], pr.at[2], pool_s.at[2], pool_r.at[2], core_peer)
     lax.fori_loop(0, tiles // 2, functools.partial(last, 0), 0)
     exchanges[BX3][0]()
     exchanges[EX3 + 1][1]()
@@ -874,10 +892,10 @@
     q_ws = [
         reducer(
             2 + i,
-            lambda z, y, x, c, h, i=i: gws.at[3 * i : 3 * i + 3, z, y, x, c, :, half(h, mid)],
-            lambda z, y, x, h, i=i: fc_ws.at[3 * i : 3 * i + 3, z, y, x, :, half(h, mid)],
-            lambda h, i=i: f3_ws.at[h, 3 * i : 3 * i + 3],
-            lambda h, i=i: f2_ws.at[h, 3 * i : 3 * i + 3],
+            lambda z, y, x, c, h, i=i: gws.at[3 * i : 3 * i + 3, z, y, x, c, :, uneven(h, mid)],
+            lambda z, y, x, h, i=i: fc_ws.at[3 * i : 3 * i + 3, z, y, x, :, uneven(h, mid)],
+            lambda h, i=i: f3_ws.at[3 * i : 3 * i + 3, :, :, :, uneven(h, mid)],
+            lambda h, i=i: f2_ws.at[3 * i : 3 * i + 3, :, :, uneven(h, mid)],
             lambda k, i=i: fz_ws.at[k, 3 * i : 3 * i + 3],
         )
         for i in range(3)
@@ -897,11 +915,16 @@
 
     exchanges[BX3][1]()
     merge_grads(bx3.at[0], tot3)
-    lax.fori_loop(0, tiles, grad_three, 0)
+    pool_core.wait_recv()
+    pb[mine] = (pf[mine] + pr[0].astype(F32)).astype(BF)
+    pool_chip.start()
+    for j in range(tiles):
+        grad_three(j, 0)
     q_first.start()
     exchanges[BX3 + 1][1]()
     merge_grads(bx3.at[1], tot3, wide // 2)
-    lax.fori_loop(tiles, 2 * tiles, grad_three, 0)
+    for j in range(tiles, 2 * tiles):
+        grad_three(j, 0)
     q_we.start()
     q_first.stage2()
 
@@ -943,11 +966,6 @@
         grad_act(ghs, a2, mi2, 2, bx2, j)
     exchanges[BX2][0]()
     q_we.stage2()
-    pool_core.wait()
-    pf[...] = pf[...] + pr[0].astype(F32)
-    pb[...] = pf[...].astype(BF)
-    pool_chip = remote(pb, pr.at[1], pool_s.at[1], pool_r.at[1], chip_peer)
-    pool_chip.start()
     exchanges[BX2][1]()
     merge_grads(bx2, tot2)
 
@@ -970,7 +988,6 @@
 
     grad_taps(0)
     q_ws[0].start()
-    q_first.stage3()
     grad_taps(1)
     q_ws[1].start()
     q_ws[0].stage2()
@@ -978,7 +995,6 @@
     grad_taps(2)
     q_ws[2].start()
     q_ws[1].stage2()
-    q_first.stage4()
     rim_d[1]()
 
     def conv2_back(dy):
@@ -991,17 +1007,22 @@
             gact[j] = part_sum if dy == 0 else gact[j] + part_sum
 
     conv2_back(0)
+    q_first.stage3()
+    q_ws[2].stage2()
+    pool_chip.wait_recv()
+    conv2_back(1)
+    pool_chip.wait_send()
+    pb[mine] = (pb[mine].astype(F32) + pr[1].astype(F32)).astype(BF)
+    pool_back.start()
     q_ws[0].stage3()
-    q_ws[2].stage2()
-    conv2_back(1)
     q_we.stage4()
     conv2_back(2)
     for j in range(mid // TILE):
         ghs.j = j
         grad_act(ghs, a1, mi1, 0, bx1, j)
     exchanges[BX1][0]()
+    q_first.stage4()
     q_ws[1].stage3()
-    gwe_o[:, 0:part] = q_first.finish()
     exchanges[BX1][1]()
     merge_grads(bx1, tot1)
 
@@ -1014,8 +1035,6 @@
         gwr[t // 2, t % 2] = block.reshape(gwr.shape[2:])
     for q in q_wr:
         q.start()
-    q_ws[0].stage4()
-    q_ws[2].stage3()
 
     n_dev = n_dp * n_rows
 
@@ -1054,6 +1073,10 @@
 
     for d in range(1, n_dp):
         small_cp(d, False).start()
+    q_wr[0].stage2()
+    q_wr[1].stage2()
+    q_ws[0].stage4()
+    q_ws[2].stage3()
 
     def grad_in(j):
         cols, slot = lanes(j), j % 2
@@ -1067,27 +1090,27 @@
         for cp in out_copies(j, slot, gv_h, gc_h):
             cp.start()
 
-    q_wr[0].stage2()
-    q_wr[1].stage2()
     grad_in(0)
     grad_in(1)
     q_ws[1].stage4()
+    q_wr[0].stage3()
     grad_in(2)
-    q_wr[0].stage3()
     q_wr[1].stage3()
+    q_ws[2].stage4()
     grad_in(3)
-    q_ws[2].stage4()
     grad_in(4)
     q_wr[0].stage4()
     q_wr[1].stage4()
     for j in range(5, wide // TILE):
         grad_in(j)
+    gwe_o[:, 0:part] = q_first.finish()
     gwe_o[:, part:wide] = q_we.finish()
     gws_o[0:3] = q_ws[0].finish()
-    pool_chip.wait()
+    pool_core.wait_send()
+    pool_back.wait_recv()
+    pb[others] = pr[2]
     for out, at, maps, valid in ((poolv_o, 0, maps_v, valid_v), (poolc_o, maps_v, maps_c, valid_c)):
-        total = pf[at : at + maps] + pr[1, at : at + maps].astype(F32)
-        out[...] = (total * (1.0 / valid)).reshape(out.shape)
+        out[...] = (pb[at : at + maps].astype(F32) * (1.0 / valid)).reshape(out.shape)
     total = sb[me.dp]
     for d in range(1, n_dp):
         small_cp(d, True).wait_recv()
@@ -1098,6 +1121,7 @@
     for i, q in enumerate(q_wr):
         gwr_o[i * few : (i + 1) * few] = q.finish()
 
+    pool_back.wait_send()
     for j in (wide // TILE - 2, wide // TILE - 1):
         for cp in out_copies(j, j % 2, gv_h, gc_h):
             cp.wait()
@@ -1166,6 +1190,7 @@
     D = pltpu.SemaphoreType.DMA
 
     scratch = [
+        V((s_wr, mid), F32), V((9, s_we, mid), F32), V((s_we, wide), F32),
         V(grid4 + (s_wr, mid), BF), V((9,) + grid4 + (s_we, mid), BF), V(grid4 + (s_we, wide), BF),
         V(grid4 + (8, 128), F32),
         V((pix, 128), F32), V((cols_v, maps_v, 2, wide), BF), V((img, cols_c, crops, wide), BF),
@@ -1178,8 +1203,8 @@
         V((pix, mid), BF), V((mid, pix), BF), V((pix, mid), BF),
         V(grid4 + (s_wr, mid), BF), V((9,) + grid4 + (s_we, mid), BF), V(grid4 + (s_we, wide), BF),
         V((nz, 2, nx, s_we, wide), BF), V((9, nz, 2, nx, s_we, mid), BF), V((nz, 2, nx, s_wr, mid), BF),
-        V((2, nz, 2, s_we, wide // 4), BF), V((2, 9, nz, 2, s_we, mid // 2), BF), V((2, nz, 2, s_wr, mid // 2), BF),
-        V((2, nz, s_we, wide // 4), BF), V((2, 9, nz, s_we, mid // 2), BF), V((2, nz, s_wr, mid // 2), BF),
+        V((2, nz, 2, s_we, wide // 4), BF), V((9, nz, 2, s_we, mid), BF), V((2, nz, 2, s_wr, mid // 2), BF),
+        V((2, nz, s_we, wide // 4), BF), V((9, nz, s_we, mid), BF), V((2, nz, s_wr, mid // 2), BF),
         V((nz - 1, s_we, wide // 2), BF), V((nz - 1, 9, s_we, mid), BF), V((nz - 1, s_wr, mid), BF),
         V((nz - 1, 2, nx, s_we, wide // 2), BF), V((2, s_we, wide // 4), BF), V((2, s_we, wide // 2), BF),
         V((8, mid), F32), V((8, wide), F32),
@@ -1188,10 +1213,10 @@
         V((n_rows, 8, mid // 2), F32), V((n_rows, 8, mid // 2), F32), V((2, n_rows, 8, wide // 4), F32),
         V((n_rows, 8, mid // 2), F32), V((n_rows, 8, mid // 2), F32), V((2, n_rows, 8, wide // 4), F32),
         V((4, mid), F32), V((4, mid), F32), V((4, wide), F32),
-        V((maps_v + maps_c, wide), F32), V((maps_v + maps_c, wide), BF), V((2, maps_v + maps_c, wide), BF),
+        V((maps_v + maps_c, wide), F32), V((maps_v + maps_c, wide), BF), V((3, (maps_v + maps_c) // 2, wide), BF),
         V((n_dp, 8, 128), F32), V((n_dp - 1, 8, 128), F32),
-        D((3, cols_v + 1)), D((2, 2)), D((7, 5 * nz + 4)), D((7, 5 * nz + 4)), D((7, 6 + nz)), D((7, 6 + nz)),
-        D((9, n_rows - 1)), D((9, n_rows - 1)), D((2, 4)), D((2, 4)), D((2,)), D((2,)), D((n_dp - 1,)), D((n_dp - 1,)),
+        D((3, max(cols_v + 1, 5))), D((2, 2)), D((7, 5 * nz + 4)), D((7, 5 * nz + 4)), D((7, 6 + nz)), D((7, 6 + nz)),
+        D((9, n_rows - 1)), D((9, n_rows - 1)), D((2, 4)), D((2, 4)), D((3,)), D((3,)), D((n_dp - 1,)), D((n_dp - 1,)),
     ]
     out_v = jax.ShapeDtypeStruct((maps_v, cols_v, 2, wide), F32)
     out_c = jax.ShapeDtypeStruct((maps_c, cols_c, wide // TILE, TILE // 128, 128), F32)
@@ -1203,7 +1228,7 @@
             jax.ShapeDtypeStruct((s_wr, mid), F32), jax.ShapeDtypeStruct((9, s_we, mid), F32),
             jax.ShapeDtypeStruct((s_we, wide), F32), jax.ShapeDtypeStruct((8, 128), F32),
         ],
-        in_specs=[hbm] * 6 + [vm] * 11,
+        in_specs=[hbm] * 9 + [vm] * 8,
         out_specs=[hbm] * 4 + [vm] * 6,
         scratch_shapes=scratch,
         compiler_params=pltpu.CompilerParams(
@@ -1211,7 +1236,7 @@
         ),
     )(
         views_in(xv), crops_in(xc), views_in(cv), crops_in(cc), cpv, cpc,
-        mv.transpose(1, 2, 0), mc.transpose(1, 2, 0), wr, ws.reshape(9, s_we, mid), we,
+        wr, ws.reshape(9, s_we, mid), we, mv.transpose(1, 2, 0), mc.transpose(1, 2, 0),
         g1.reshape(1, -1), s1.reshape(1, -1), g2.reshape(1, -1), s2.reshape(1, -1),
         g3.reshape(1, -1), s3.reshape(1, -1),
     )

time: 151 us -> 137 us (0.907)
  Pallas kernels: 150 us -> 136 us
    pallas_call x1, Pallas kernels: 139 us -> 125 us  [block_step(): pl.pallas_call(functools.partial(kernel, n_dp, n_rows, (maps_v, cols_v, m...]
where the time goes in v2:
time: 137 us
  Pallas kernels  136 us (99%)
    pallas_call x1, Pallas kernels, block_step(): pl.pallas_call(functools.partial(kernel, n_dp, n_rows, (maps_v, cols_v, m...  125 us
    pallas_call x1, Pallas kernels, block_step(): pl.pallas_call(hand_over, out_shape=shapes + [jax.ShapeDtypeStruct((1, w)...  10.5 us

profile of v2, /device:TPU:0, one launch (start us, length us, event | category | flops | bytes accessed | tf_op | source)
XLA Modules:
  0.0 136.7 jit_solution(14566053749300558627)
XLA Ops:
  0.7 125.4 %shard_map.280 = (f32[32,7,2,2048]{3,2,1,0:T(2,128)}, f32[64,3,8,2,128]{4,3,2,1,0:T(2,128)}, f32[32,7,2,2048]{3,2,1,0:T(2,128)}, f32[64,3,8,2,128]{4,3,2,1,0:T(2...) custom-call(bf16[32,7,2,2048]{3,2,1,0:T(2,128)(2,1)} %bitcast.40, ...), custom_call_target="tpu_custom_call" | custom-call | tf_op jit(solution)/shard_map/pallas_call | solution.py:1223
  126.1 10.5 %shard_map.281 = (f32[32,7,2,2048]{3,2,1,0:T(2,128)}, f32[64,3,8,2,128]{4,3,2,1,0:T(2,128)}, f32[32,7,2,2048]{3,2,1,0:T(2,128)}, f32[64,3,8,2,128]{4,3,2,1,0:T(2...) custom-call(f32[32,7,2,2048]{3,2,1,0:T(2,128)} %get-tuple-element.40, ...), custom_call_target="tpu_custom_call" | custom-call | tf_op jit(solution)/shard_map/pallas_call | solution.py:1246

commit v3 on v2

--- a/solution.py
+++ b/solution.py
@@ -180,59 +180,6 @@
     def finish(self):
         for k in range(self.me.nz):
             self.wait(4 + self.me.nz + k, self.source(k), ALL, ALL, None, 1 - self.me.c)
-
-
-class ReducePlane(Piece):
-    def __init__(self, me, view, from_core, from_z, from_diagonal, from_xy, ssem, rsem):
-        super().__init__(me, view, ssem, rsem)
-        self.fc, self.fz, self.fd, self.fxy = from_core, from_z, from_diagonal, from_xy
-        self.DG, self.H = me.nz, me.nz + 2
-
-    def start(self):
-        c = self.me.c
-        self.send(0, self.view(ALL, ALL, ALL, 1 - c, None), self.fc(), self.pc)
-
-    def stage2(self):
-        me = self.me
-        self.got(0, self.fc())
-        ref = self.view(ALL, ALL, ALL, me.c, None)
-        ref[...] = ref[...] + self.fc()[...]
-        for k in range(1, me.nz):
-            z = (me.z + k) % me.nz
-            self.send(k, self.view(z, ALL, ALL, me.c, None), self.fz(k - 1), self.pz(k))
-
-    def stage3(self):
-        me = self.me
-        ref = self.view(me.z, ALL, ALL, me.c, None)
-        total = ref[...].astype(F32)
-        for k in range(1, me.nz):
-            self.got(k, self.fz(k - 1))
-            total = total + self.fz(k - 1)[...].astype(F32)
-        ref[...] = total.astype(BF)
-        self.send(self.DG, self.view(me.z, 1 - me.y, 1 - me.x, me.c, 0), self.fd(0), self.px)
-        self.send(self.DG + 1, self.view(me.z, 1 - me.y, 1 - me.x, me.c, 1), self.fd(1), self.py)
-        self.send(self.H, self.view(me.z, me.y, 1 - me.x, me.c, 0), self.fxy(0, 0), self.px)
-        self.send(self.H + 1, self.view(me.z, 1 - me.y, me.x, me.c, 1), self.fxy(1, 1), self.py)
-
-    def stage4(self):
-        me = self.me
-        self.got(self.DG, self.fd(0))
-        ref = self.view(me.z, 1 - me.y, me.x, me.c, 0)
-        ref[...] = ref[...] + self.fd(0)[...]
-        self.send(self.H + 2, ref, self.fxy(1, 0), self.py)
-        self.got(self.DG + 1, self.fd(1))
-        ref = self.view(me.z, me.y, 1 - me.x, me.c, 1)
-        ref[...] = ref[...] + self.fd(1)[...]
-        self.send(self.H + 3, ref, self.fxy(0, 1), self.px)
-
-    def finish(self):
-        me = self.me
-        self.got(self.H, self.fxy(0, 0))
-        self.got(self.H + 1, self.fxy(1, 1))
-        self.got(self.H + 2, self.fxy(1, 0))
-        self.got(self.H + 3, self.fxy(0, 1))
-        total = self.view(me.z, me.y, me.x, me.c, None)[...].astype(F32)
-        return total + self.fxy(0, None)[...].astype(F32) + self.fxy(1, None)[...].astype(F32)
 
 
 class Reduce:
@@ -335,7 +282,7 @@
         yv_h, yc_h, gv_h, gc_h, poolv_o, poolc_o, gwr_o, gws_o, gwe_o, small_o,
         wr_in, ws_in, we_in, wr, ws, we, par, mask, raw_v, raw_c, cpv, cpc, x, xt, cot, a1, a2, a3, gpre, ysv, ysc, gact,
         hv, hc, dv, dc, h2, h2t, ga1, gwr, gws, gwe,
-        fc_we, fc_ws, fc_wr, f3_we, f3_ws, f3_wr, f2_we, f2_ws, f2_wr, fz_we, fz_ws, fz_wr, fp_we, fd_we, fh_we,
+        fc_we, fc_ws, fc_wr, f3_we, f3_ws, f3_wr, f2_we, f2_ws, f2_wr, fz_we, fz_ws, fz_wr,
         p1, p3, mi1, mi2, mi3, cnt, ex1, ex2, ex3, bx1, bx2, bx3, tot1, tot2, tot3,
         pf, pb, pr, sb, rb,
         in_sem, out_sem, ag_s, ag_r, rs_s, rs_r, ex_s, ex_r, halo_s, halo_r, pool_s, pool_r, sm_s, sm_r,
@@ -708,8 +655,6 @@
     pieces[3].diagonal()
     pieces[2].last()
     pieces[1].finish()
-    rim_h[1]()
-
     def windows(v, c, dy, dx):
         left = [v[r + dy, dx * maps_v : dx * maps_v + row_v, :] for r in (0, 1)]
         return jnp.concatenate(left + [c[dy, dx * maps_c : dx * maps_c + row_c, :]], axis=0)
@@ -719,12 +664,13 @@
         for j in range(mid // TILE):
             w = ws[3 * dy : 3 * dy + 3, :, :, :, :, :, lanes(j)].reshape(3 * mid, TILE)
             part_sum = dot(left, w)
-            a2[:, lanes(j)] = part_sum if dy == 0 else a2[:, lanes(j)] + part_sum
-
-    conv2(0)
-    pieces[4].diagonal()
+            a2[:, lanes(j)] = part_sum if dy == 1 else a2[:, lanes(j)] + part_sum
+
     pieces[2].finish()
     conv2(1)
+    pieces[4].diagonal()
+    rim_h[1]()
+    conv2(0)
     pieces[3].last()
     pieces[3].finish()
     conv2(2)
@@ -867,28 +813,20 @@
         )
         return carry
 
-    q_first = ReducePlane(
-        me,
-        lambda z, y, x, c, h: gwe.at[z, y, x, c, :, half(h, part, 0, part)],
-        lambda: fc_we.at[:, :, :, :, 0:part],
-        lambda k: fp_we.at[k],
-        lambda h: fd_we.at[h],
-        lambda k, h: fh_we.at[k, :, half(h, part)],
-        rs_s.at[0],
-        rs_r.at[0],
-    )
-
     def reducer(k, view, fc, f3, f2, fz):
         return Reduce(me, view, fc, f3, f2, fz, rs_s.at[k], rs_r.at[k])
 
-    q_we = reducer(
-        1,
-        lambda z, y, x, c, h: gwe.at[z, y, x, c, :, half(h, part, part, part)],
-        lambda z, y, x, h: fc_we.at[z, y, x, :, half(h, part, part, part)],
-        lambda h: f3_we.at[h],
-        lambda h: f2_we.at[h],
-        lambda k: fz_we.at[k],
-    )
+    q_we = [
+        reducer(
+            i,
+            lambda z, y, x, c, h, at=i * part: gwe.at[z, y, x, c, :, half(h, part, at, part)],
+            lambda z, y, x, h, at=i * part: fc_we.at[z, y, x, :, half(h, part, at, part)],
+            lambda h, i=i: f3_we.at[i, h],
+            lambda h, i=i: f2_we.at[i, h],
+            lambda k, i=i: fz_we.at[i, k],
+        )
+        for i in range(2)
+    ]
     q_ws = [
         reducer(
             2 + i,
@@ -915,18 +853,15 @@
 
     exchanges[BX3][1]()
     merge_grads(bx3.at[0], tot3)
-    pool_core.wait_recv()
-    pb[mine] = (pf[mine] + pr[0].astype(F32)).astype(BF)
-    pool_chip.start()
     for j in range(tiles):
         grad_three(j, 0)
-    q_first.start()
+    q_we[0].start()
     exchanges[BX3 + 1][1]()
     merge_grads(bx3.at[1], tot3, wide // 2)
+    q_we[0].stage2()
     for j in range(tiles, 2 * tiles):
         grad_three(j, 0)
-    q_we.start()
-    q_first.stage2()
+    q_we[1].start()
 
     def grad_act(gh, a, mi, i, buf, j):
         cols = lanes(j)
@@ -965,7 +900,9 @@
         ghs.j = j
         grad_act(ghs, a2, mi2, 2, bx2, j)
     exchanges[BX2][0]()
-    q_we.stage2()
+    q_we[1].stage2()
+    pool_core.wait_recv()
+    pb[mine] = (pf[mine] + pr[0].astype(F32)).astype(BF)
     exchanges[BX2][1]()
     merge_grads(bx2, tot2)
 
@@ -979,23 +916,13 @@
 
     grad_norm_all(a2, mi2, tot2, 2, lambda s, cols, value: store_rows(dv, dc, s, cols, value))
     rim_d[0]()
+    q_we[0].stage3()
 
     def grad_taps(dy):
         right = windows(dv, dc, 1, 1)
         for dx in range(3):
             total = dot_r(windows(hv, hc, dy, dx), right)
             gws[3 * dy + dx] = total.astype(BF).reshape(gws.shape[1:])
-
-    grad_taps(0)
-    q_ws[0].start()
-    grad_taps(1)
-    q_ws[1].start()
-    q_ws[0].stage2()
-    q_we.stage3()
-    grad_taps(2)
-    q_ws[2].start()
-    q_ws[1].stage2()
-    rim_d[1]()
 
     def conv2_back(dy):
         left = jnp.concatenate([windows(dv, dc, 2 - dy, 2 - dx) for dx in range(3)], axis=1)
@@ -1004,25 +931,28 @@
                 [tile_rows(ws.at[3 * dy + dx], j).reshape(TILE, mid) for dx in range(3)], axis=1
             )
             part_sum = dot_t(left, w)
-            gact[j] = part_sum if dy == 0 else gact[j] + part_sum
-
+            gact[j] = part_sum if dy == 1 else gact[j] + part_sum
+
+    grad_taps(0)
+    q_ws[0].start()
+    conv2_back(1)
+    grad_taps(1)
+    q_ws[1].start()
+    q_ws[0].stage2()
+    q_we[1].stage3()
+    q_we[0].stage4()
+    rim_d[1]()
     conv2_back(0)
-    q_first.stage3()
-    q_ws[2].stage2()
-    pool_chip.wait_recv()
-    conv2_back(1)
-    pool_chip.wait_send()
-    pb[mine] = (pb[mine].astype(F32) + pr[1].astype(F32)).astype(BF)
-    pool_back.start()
-    q_ws[0].stage3()
-    q_we.stage4()
+    q_ws[1].stage2()
     conv2_back(2)
     for j in range(mid // TILE):
         ghs.j = j
         grad_act(ghs, a1, mi1, 0, bx1, j)
     exchanges[BX1][0]()
-    q_first.stage4()
-    q_ws[1].stage3()
+    grad_taps(2)
+    q_ws[2].start()
+    q_we[1].stage4()
+    q_ws[0].stage3()
     exchanges[BX1][1]()
     merge_grads(bx1, tot1)
 
@@ -1035,6 +965,11 @@
         gwr[t // 2, t % 2] = block.reshape(gwr.shape[2:])
     for q in q_wr:
         q.start()
+    q_ws[2].stage2()
+    q_ws[1].stage3()
+    q_wr[0].stage2()
+    q_wr[1].stage2()
+    q_ws[0].stage4()
 
     n_dev = n_dp * n_rows
 
@@ -1073,10 +1008,8 @@
 
     for d in range(1, n_dp):
         small_cp(d, False).start()
-    q_wr[0].stage2()
-    q_wr[1].stage2()
-    q_ws[0].stage4()
     q_ws[2].stage3()
+    q_ws[1].stage4()
 
     def grad_in(j):
         cols, slot = lanes(j), j % 2
@@ -1092,19 +1025,23 @@
 
     grad_in(0)
     grad_in(1)
-    q_ws[1].stage4()
     q_wr[0].stage3()
     grad_in(2)
     q_wr[1].stage3()
+    pool_chip.start()
     q_ws[2].stage4()
     grad_in(3)
     grad_in(4)
     q_wr[0].stage4()
     q_wr[1].stage4()
+    pool_chip.wait_send()
+    pool_chip.wait_recv()
+    pb[mine] = (pb[mine].astype(F32) + pr[1].astype(F32)).astype(BF)
+    pool_back.start()
     for j in range(5, wide // TILE):
         grad_in(j)
-    gwe_o[:, 0:part] = q_first.finish()
-    gwe_o[:, part:wide] = q_we.finish()
+    gwe_o[:, part:wide] = q_we[1].finish()
+    gwe_o[:, 0:part] = q_we[0].finish()
     gws_o[0:3] = q_ws[0].finish()
     pool_core.wait_send()
     pool_back.wait_recv()
@@ -1132,7 +1069,7 @@
         e[2]()
     rim_h[2]()
     rim_d[2]()
-    for q in [q_first, q_we] + q_ws + q_wr:
+    for q in q_we + q_ws + q_wr:
         q.drain()
     for d in range(1, n_dp):
         small_cp(d, False).wait_send()
@@ -1203,10 +1140,9 @@
         V((pix, mid), BF), V((mid, pix), BF), V((pix, mid), BF),
         V(grid4 + (s_wr, mid), BF), V((9,) + grid4 + (s_we, mid), BF), V(grid4 + (s_we, wide), BF),
         V((nz, 2, nx, s_we, wide), BF), V((9, nz, 2, nx, s_we, mid), BF), V((nz, 2, nx, s_wr, mid), BF),
-        V((2, nz, 2, s_we, wide // 4), BF), V((9, nz, 2, s_we, mid), BF), V((2, nz, 2, s_wr, mid // 2), BF),
-        V((2, nz, s_we, wide // 4), BF), V((9, nz, s_we, mid), BF), V((2, nz, s_wr, mid // 2), BF),
-        V((nz - 1, s_we, wide // 2), BF), V((nz - 1, 9, s_we, mid), BF), V((nz - 1, s_wr, mid), BF),
-        V((nz - 1, 2, nx, s_we, wide // 2), BF), V((2, s_we, wide // 4), BF), V((2, s_we, wide // 2), BF),
+        V((2, 2, nz, 2, s_we, wide // 4), BF), V((9, nz, 2, s_we, mid), BF), V((2, nz, 2, s_wr, mid // 2), BF),
+        V((2, 2, nz, s_we, wide // 4), BF), V((9, nz, s_we, mid), BF), V((2, nz, s_wr, mid // 2), BF),
+        V((2, nz - 1, s_we, wide // 2), BF), V((nz - 1, 9, s_we, mid), BF), V((nz - 1, s_wr, mid), BF),
         V((8, mid), F32), V((8, wide), F32),
         V((4, mid), F32), V((4, mid), F32), V((4, wide), F32),
         V((n_rows, 8, 128), F32),

time: 137 us -> 136 us (level)
  no operation moved by 1% of the time
where the time goes in v3:
time: 136 us
  Pallas kernels  135 us (99%)
    pallas_call x1, Pallas kernels, block_step(): pl.pallas_call(functools.partial(kernel, n_dp, n_rows, (maps_v, cols_v, m...  124 us
    pallas_call x1, Pallas kernels, block_step(): pl.pallas_call(hand_over, out_shape=shapes + [jax.ShapeDtypeStruct((1, w)...  10.5 us

profile of v3, /device:TPU:0, one launch (start us, length us, event | category | flops | bytes accessed | tf_op | source)
XLA Modules:
  0.0 135.6 jit_solution(196020234007645161)
XLA Ops:
  0.7 124.3 %shard_map.280 = (f32[32,7,2,2048]{3,2,1,0:T(2,128)}, f32[64,3,8,2,128]{4,3,2,1,0:T(2,128)}, f32[32,7,2,2048]{3,2,1,0:T(2,128)}, f32[64,3,8,2,128]{4,3,2,1,0:T(2...) custom-call(bf16[32,7,2,2048]{3,2,1,0:T(2,128)(2,1)} %bitcast.40, ...), custom_call_target="tpu_custom_call" | custom-call | tf_op jit(solution)/shard_map/pallas_call | solution.py:1159
  124.9 10.5 %shard_map.281 = (f32[32,7,2,2048]{3,2,1,0:T(2,128)}, f32[64,3,8,2,128]{4,3,2,1,0:T(2,128)}, f32[32,7,2,2048]{3,2,1,0:T(2,128)}, f32[64,3,8,2,128]{4,3,2,1,0:T(2...) custom-call(f32[32,7,2,2048]{3,2,1,0:T(2,128)} %get-tuple-element.40, ...), custom_call_target="tpu_custom_call" | custom-call | tf_op jit(solution)/shard_map/pallas_call | solution.py:1182

commit v4 on v3

--- a/solution.py
+++ b/solution.py
@@ -279,8 +279,8 @@
     (
         xv_h, xc_h, cv_h, cc_h, cpv_h, cpc_h, wr_h, ws_h, we_h, mv_in, mc_in,
         g1_in, s1_in, g2_in, s2_in, g3_in, s3_in,
-        yv_h, yc_h, gv_h, gc_h, poolv_o, poolc_o, gwr_o, gws_o, gwe_o, small_o,
-        wr_in, ws_in, we_in, wr, ws, we, par, mask, raw_v, raw_c, cpv, cpc, x, xt, cot, a1, a2, a3, gpre, ysv, ysc, gact,
+        yv_h, yc_h, gv_h, gc_h, poolv_h, poolc_h, gwe_h, gwr_o, gws_o, small_o,
+        poolv_o, poolc_o, gwe_o, res_sem, wr_in, ws_in, we_in, wr, ws, we, par, mask, raw_v, raw_c, cpv, cpc, x, xt, cot, a1, a2, a3, gpre, ysv, ysc, gact,
         hv, hc, dv, dc, h2, h2t, ga1, gwr, gws, gwe,
         fc_we, fc_ws, fc_wr, f3_we, f3_ws, f3_wr, f2_we, f2_ws, f2_wr, fz_we, fz_ws, fz_wr,
         p1, p3, mi1, mi2, mi3, cnt, ex1, ex2, ex3, bx1, bx2, bx3, tot1, tot2, tot3,
@@ -935,15 +935,15 @@
 
     grad_taps(0)
     q_ws[0].start()
-    conv2_back(1)
     grad_taps(1)
     q_ws[1].start()
     q_ws[0].stage2()
+    conv2_back(1)
     q_we[1].stage3()
+    q_ws[1].stage2()
     q_we[0].stage4()
     rim_d[1]()
     conv2_back(0)
-    q_ws[1].stage2()
     conv2_back(2)
     for j in range(mid // TILE):
         ghs.j = j
@@ -1048,6 +1048,12 @@
     pb[others] = pr[2]
     for out, at, maps, valid in ((poolv_o, 0, maps_v, valid_v), (poolc_o, maps_v, maps_c, valid_c)):
         out[...] = (pb[at : at + maps].astype(F32) * (1.0 / valid)).reshape(out.shape)
+    results = [
+        pltpu.make_async_copy(src, dst, res_sem.at[i])
+        for i, (src, dst) in enumerate(((poolv_o, poolv_h), (poolc_o, poolc_h), (gwe_o, gwe_h)))
+    ]
+    for cp in results:
+        cp.start()
     total = sb[me.dp]
     for d in range(1, n_dp):
         small_cp(d, True).wait_recv()
@@ -1058,6 +1064,8 @@
     for i, q in enumerate(q_wr):
         gwr_o[i * few : (i + 1) * few] = q.finish()
 
+    for cp in results:
+        cp.wait()
     pool_back.wait_send()
     for j in (wide // TILE - 2, wide // TILE - 1):
         for cp in out_copies(j, j % 2, gv_h, gc_h):
@@ -1079,7 +1087,7 @@
     n = (len(refs) - 8) // 3
     srcs, small, dsts = refs[:n], refs[n], refs[n + 1 : 2 * n + 1]
     cuts, bufs, sem = refs[2 * n + 1 : 2 * n + 7], refs[2 * n + 7 : -1], refs[-1]
-    parts = 4
+    parts = 2
     ways = []
     for i, (src, buf, dst) in enumerate(zip(srcs, bufs, dsts)):
         count = parts if src.shape[0] % parts == 0 else 1
@@ -1088,18 +1096,20 @@
             rows = slice(k * per, (k + 1) * per)
             ways.append(
                 (
+                    k,
                     pltpu.make_async_copy(src.at[rows], buf.at[rows], sem.at[0, i, k]),
                     pltpu.make_async_copy(buf.at[rows], dst.at[rows], sem.at[1, i, k]),
                 )
             )
-    for inward, _ in ways:
+    ways.sort(key=lambda way: way[0])
+    for _, inward, _ in ways:
         inward.start()
     for i, ref in enumerate(cuts):
         ref[...] = small[i : i + 1, 0 : ref.shape[1]]
-    for inward, outward in ways:
+    for _, inward, outward in ways:
         inward.wait()
         outward.start()
-    for _, outward in ways:
+    for _, _, outward in ways:
         outward.wait()
 
 
@@ -1127,6 +1137,7 @@
     D = pltpu.SemaphoreType.DMA
 
     scratch = [
+        V(cpv.shape, F32), V(cpc.shape, F32), V((s_we, wide), F32), D((3,)),
         V((s_wr, mid), F32), V((9, s_we, mid), F32), V((s_we, wide), F32),
         V(grid4 + (s_wr, mid), BF), V((9,) + grid4 + (s_we, mid), BF), V(grid4 + (s_we, wide), BF),
         V(grid4 + (8, 128), F32),
@@ -1161,11 +1172,11 @@
         out_shape=[
             out_v, out_c, out_v, out_c,
             jax.ShapeDtypeStruct(cpv.shape, F32), jax.ShapeDtypeStruct(cpc.shape, F32),
-            jax.ShapeDtypeStruct((s_wr, mid), F32), jax.ShapeDtypeStruct((9, s_we, mid), F32),
-            jax.ShapeDtypeStruct((s_we, wide), F32), jax.ShapeDtypeStruct((8, 128), F32),
+            jax.ShapeDtypeStruct((s_we, wide), F32), jax.ShapeDtypeStruct((s_wr, mid), F32),
+            jax.ShapeDtypeStruct((9, s_we, mid), F32), jax.ShapeDtypeStruct((8, 128), F32),
         ],
         in_specs=[hbm] * 9 + [vm] * 8,
-        out_specs=[hbm] * 4 + [vm] * 6,
+        out_specs=[hbm] * 7 + [vm] * 3,
         scratch_shapes=scratch,
         compiler_params=pltpu.CompilerParams(
             collective_id=0, has_side_effects=True, vmem_limit_bytes=63 << 20
@@ -1187,7 +1198,7 @@
         scratch_shapes=[V(o.shape, F32) for o in big] + [D((2, len(big), 4))],
         compiler_params=pltpu.CompilerParams(vmem_limit_bytes=62 << 20),
     )(*outs)
-    yv, yc, gv, gc, pool_v, pool_c, gwr, gws, gwe = res[:9]
+    yv, yc, gv, gc, pool_v, pool_c, gwe, gwr, gws = res[:9]
     small = [r.reshape(-1) for r in res[9:]]
 
     def views_out(t):

time: 136 us -> 134 us (0.985)
  Pallas kernels: 135 us -> 133 us
where the time goes in v4:
time: 134 us
  Pallas kernels  133 us (99%)
    pallas_call x1, Pallas kernels, block_step(): pl.pallas_call(functools.partial(kernel, n_dp, n_rows, (maps_v, cols_v, m...  123 us
    pallas_call x1, Pallas kernels, block_step(): pl.pallas_call(hand_over, out_shape=shapes + [jax.ShapeDtypeStruct((1, w)...  9.68 us

profile of v4, /device:TPU:0, one launch (start us, length us, event | category | flops | bytes accessed | tf_op | source)
XLA Modules:
  0.0 134.0 jit_solution(8245331577472805630)
XLA Ops:
  0.7 123.5 %shard_map.280 = (f32[32,7,2,2048]{3,2,1,0:T(2,128)}, f32[64,3,8,2,128]{4,3,2,1,0:T(2,128)}, f32[32,7,2,2048]{3,2,1,0:T(2,128)}, f32[64,3,8,2,128]{4,3,2,1,0:T(2...) custom-call(bf16[32,7,2,2048]{3,2,1,0:T(2,128)(2,1)} %bitcast.40, ...), custom_call_target="tpu_custom_call" | custom-call | tf_op jit(solution)/shard_map/pallas_call | solution.py:1170
  124.1 9.7 %shard_map.281 = (f32[32,7,2,2048]{3,2,1,0:T(2,128)}, f32[64,3,8,2,128]{4,3,2,1,0:T(2,128)}, f32[32,7,2,2048]{3,2,1,0:T(2,128)}, f32[64,3,8,2,128]{4,3,2,1,0:T(2...) custom-call(f32[32,7,2,2048]{3,2,1,0:T(2,128)} %get-tuple-element.40, ...), custom_call_target="tpu_custom_call" | custom-call | tf_op jit(solution)/shard_map/pallas_call | solution.py:1193
